TPU v7x, 32 devices: a whole 2x2x4 slice. The times are simulated.
32 devices in a mesh: fsdp: 8 (over y, x, core), seq: 4 (over z).
Axes of the slice: x: 2, y: 2, z: 4, core: 2. Of those that a mesh axis runs over, the one named last changes fastest.
Arguments:
- inputs: float32 [4096, 768], P(('fsdp', 'seq')), may hold values from -6 to 6
- qkv_weight: bfloat16 [768, 2304], P(('fsdp', 'seq')), may hold values from -8 to 8
- proj_weight: bfloat16 [768, 768], P(('fsdp', 'seq')), may hold values from -2.5 to 2.5
- first_gain: bfloat16 [768], P(('fsdp', 'seq')), may hold values from 0.5 to 1.5
- first_shift: bfloat16 [768], P(('fsdp', 'seq')), may hold values from -3 to 3
- second_gain: bfloat16 [768], P(('fsdp', 'seq')), may hold values from 0.5 to 1.5
- second_shift: bfloat16 [768], P(('fsdp', 'seq')), may hold values from -3 to 3
- expert_up: bfloat16 [8, 768, 3072], P('fsdp', None, 'seq'), may hold values from -0.21875 to 0.21875
- expert_down: bfloat16 [8, 768, 3072], P('fsdp', None, 'seq'), may hold values from -0.109375 to 0.109375
- gate_logits: float32 [4096, 2], P(('fsdp', 'seq')), may hold values from -160 to 160
- routes: int32 [4096, 2], P(('fsdp', 'seq')), may hold values from 0 to 7, all different within a row; in each aligned block of 128 rows (0 to 127, 128 to 255, ...) at most 64 rows name the same one
- cotangent: float32 [4096, 768], P(('fsdp', 'seq')), may hold values from -6 to 6
Outputs:
- output: float32 [4096, 768], P(('fsdp', 'seq'))
- grad_inputs: float32 [4096, 768], P(('fsdp', 'seq'))
- grad_qkv_weight: float32 [768, 2304], P(('fsdp', 'seq'))
- grad_proj_weight: float32 [768, 768], P(('fsdp', 'seq'))
- grad_first_gain: float32 [768], P(('fsdp', 'seq'))
- grad_first_shift: float32 [768], P(('fsdp', 'seq'))
- grad_second_gain: float32 [768], P(('fsdp', 'seq'))
- grad_second_shift: float32 [768], P(('fsdp', 'seq'))
- grad_expert_up: float32 [8, 768, 3072], P('fsdp', None, 'seq')
- grad_expert_down: float32 [8, 768, 3072], P('fsdp', None, 'seq')
Inputs may be any that keep to these rules, and one draw needn't show every extreme that they name: `routes`: each row names 2 different experts. In each aligned block of 128 rows (the rows of one device) no expert is named by more than 64 rows, a bound that some block reaches.
All inputs are finite; a program needn't handle non-finite values.
Results may differ from a plain program's by a relative error of at most 0.012.
Values may be sent and summed in bfloat16 or wider, within the bound.
No kernel may reach another device: no remote copies, remote signals or barrier semaphores. Data moves between devices by JAX's collectives and lax.ppermute only.
A program may use at most 128 MiB of HBM per device.

v0:
```python
import functools

import jax
import jax.numpy as jnp
from jax import lax
from jax.experimental import pallas as pl
from jax.experimental.pallas import tpu as pltpu
from jax.sharding import PartitionSpec as P


HD = 64
EPS = 1e-06
BF = jnp.bfloat16
F32 = jnp.float32
C0 = 0.7978845608028654
C1 = 0.044715


def mm(a, b):
    return jnp.dot(a, b, preferred_element_type=F32)


def mm_nt(a, b):
    return lax.dot_general(a, b, (((1,), (1,)), ((), ())), preferred_element_type=F32)


def mm_tn(a, b):
    return lax.dot_general(a, b, (((0,), (0,)), ((), ())), preferred_element_type=F32)


def kernel_call(body, outs, args, smem=0, scratch=()):
    vm = pl.BlockSpec(memory_space=pltpu.VMEM)
    sm = pl.BlockSpec(memory_space=pltpu.SMEM)
    return pl.pallas_call(
        body,
        out_shape=[jax.ShapeDtypeStruct(s, d) for s, d in outs],
        in_specs=[sm] * smem + [vm] * (len(args) - smem),
        out_specs=[vm] * len(outs),
        scratch_shapes=list(scratch),
    )(*args)


def exchange(chunks, axis, count, stride=1):
    got = [chunks[0]]
    for d in range(stride, count, stride):
        got.append(lax.ppermute(chunks[d // stride], axis, [(i, i ^ d) for i in range(count)]))
    return got


def swap(x, axis):
    return lax.all_to_all(x, axis, split_axis=0, concat_axis=0, tiled=True)


def after(x, *others):
    return lax.optimization_barrier((x, *others))[0]


def norm_stats(x):
    mean = jnp.mean(x, axis=-1, keepdims=True)
    centred = x - mean
    spread = jnp.mean(centred * centred, axis=-1, keepdims=True)
    return mean, centred, spread


def norm_parts(x):
    _, centred, spread = norm_stats(x)
    scale = lax.rsqrt(spread + EPS)
    return centred * scale, scale


def norm_back(hat, scale, gain, dy):
    dhat = dy * gain
    a = jnp.mean(dhat, axis=-1, keepdims=True)
    b = jnp.mean(dhat * hat, axis=-1, keepdims=True)
    return scale * (dhat - a - hat * b)


INFO = 8


def prepare_body(x_ref, cot_ref, info_ref, hat_ref, pack_ref):
    rows = x_ref.shape[0]
    mean, centred, spread = norm_stats(x_ref[...])
    scale = lax.rsqrt(spread + EPS)
    hat_ref[...] = (centred * scale).astype(BF)
    pack_ref[:rows, :] = cot_ref[...].astype(BF)
    lane = lax.broadcasted_iota(jnp.int32, info_ref.shape, 1)
    table = jnp.where(lane == 4, mean, jnp.where(lane == 5, scale, info_ref[...]))
    table = table.T[:INFO, :]
    high = table.astype(BF)
    rest = table - high.astype(F32)
    middle = rest.astype(BF)
    low = (rest - middle.astype(F32)).astype(BF)
    pack_ref[rows:, :] = jnp.zeros((pack_ref.shape[0] - rows, pack_ref.shape[1]), BF)
    span = table.shape[1]
    pack_ref[rows:, :span] = jnp.concatenate([high, middle], axis=0)
    pack_ref[rows:, span : 2 * span] = jnp.concatenate([low, jnp.zeros_like(low)], axis=0)


def table_body(experts, me_ref, *refs):
    blocks = refs[:-4]
    pos_ref, gate_ref, stat_ref, all_ref = refs[-4:]
    count = len(blocks)
    rows = blocks[0].shape[0] - 2 * INFO
    for d in range(count):
        first = blocks[d][rows:, :rows].astype(F32)
        second = blocks[d][rows:, rows : 2 * rows].astype(F32)
        values = first[:INFO, :] + first[INFO:, :] + second[:INFO, :]
        all_ref[me_ref[1] ^ d] = values
        wide = jnp.concatenate([values, jnp.zeros((rows - INFO, rows), F32)], axis=0)
        stat_ref[me_ref[1] ^ d] = wide.T
    flat = jnp.concatenate([all_ref[j] for j in range(count)], axis=1)
    tokens = flat.shape[1]
    first, second = flat[0:1, :], flat[1:2, :]
    left, right = flat[2:3, :], flat[3:4, :]
    top = jnp.maximum(left, right)
    left, right = jnp.exp(left - top), jnp.exp(right - top)
    total = left + right
    left, right = left / total, right / total
    label = lax.broadcasted_iota(jnp.int32, (experts, tokens), 0).astype(F32)
    is_first, is_second = label == first, label == second
    hit = is_first | is_second
    earlier = lax.broadcasted_iota(jnp.int32, (tokens, tokens), 0) < lax.broadcasted_iota(
        jnp.int32, (tokens, tokens), 1
    )
    rank = mm(jnp.where(hit, 1.0, 0.0).astype(BF), jnp.where(earlier, 1.0, 0.0).astype(BF))
    pos_ref[...] = jnp.where(hit, rank, -1.0)
    gate_ref[...] = jnp.where(is_first, left, 0.0) + jnp.where(is_second, right, 0.0)


def selection(pos_row, slots):
    tokens = pos_row.shape[1]
    slot = lax.broadcasted_iota(jnp.int32, (slots, tokens), 0).astype(F32)
    return slot == pos_row


def one_hot(pos_row, slots):
    return jnp.where(selection(pos_row, slots), 1.0, 0.0).astype(BF)


def dispatch_grad_body(experts, count, me_ref, pos_ref, gate_ref, *refs):
    blocks = refs[:count]
    out_ref, tok_ref = refs[count:]
    rows = blocks[0].shape[0] - 2 * INFO
    slots = out_ref.shape[1]
    for d in range(count):
        start = pl.multiple_of((me_ref[1] ^ d) * rows, rows)
        tok_ref[pl.ds(start, rows), :] = blocks[d][:rows, :]

    def step(e, carry):
        chosen = selection(pos_ref[pl.ds(e, 1), :], slots)
        pick = jnp.where(chosen, 1.0, 0.0).astype(BF)
        gate = jnp.sum(jnp.where(chosen, gate_ref[pl.ds(e, 1), :], 0.0), axis=1, keepdims=True)
        out_ref[e] = (mm(pick, tok_ref[...]) * gate).astype(BF)
        return carry

    lax.fori_loop(0, experts, step, 0)


def attention_forward_body(heads, me_ref, gains_ref, w_ref, *refs):
    blocks = refs[:-5]
    hat_ref, a_ref, qkv_ref, out_ref, lse_ref = refs[-5:]
    rows = blocks[0].shape[0]
    group = heads * HD
    for d in range(len(blocks)):
        start = pl.multiple_of((me_ref[1] ^ d) * rows, rows)
        hat_ref[pl.ds(start, rows), :] = blocks[d][...]
        a_ref[pl.ds(start, rows), :] = (
            blocks[d][...].astype(F32) * gains_ref[0:1, :] + gains_ref[1:2, :]
        ).astype(BF)
    qkv_ref[...] = mm(a_ref[...], w_ref[...]).astype(BF)
    for h in range(heads):
        q = qkv_ref[:, h * HD : (h + 1) * HD]
        k = qkv_ref[:, group + h * HD : group + (h + 1) * HD]
        v = qkv_ref[:, 2 * group + h * HD : 2 * group + (h + 1) * HD]
        scores = mm_nt(q, k) * HD ** (-0.5)
        top = jnp.max(scores, axis=-1, keepdims=True)
        weights = jnp.exp(scores - top)
        total = jnp.sum(weights, axis=-1, keepdims=True)
        probs = (weights / total).astype(BF)
        out_ref[:, h * HD : (h + 1) * HD] = mm(probs, v).astype(BF)
        lse_ref[:, h : h + 1] = top + jnp.log(total)


def attention_backward_body(heads, *refs):
    me_ref, own_ref = refs[:2]
    got = refs[2:-14]
    qkv_ref, lse_ref, w_ref, hat_ref, stat_ref, gains_ref, res_ref = refs[-14:-7]
    gqkv_ref, sums_ref, keep_ref = refs[-7:-4]
    send = refs[-4:-1]
    part_ref = refs[-1]
    group = heads * HD
    scale = HD ** (-0.5)
    grad_heads = own_ref[...]
    for ref in got:
        grad_heads = grad_heads + ref[...].astype(F32)
    grad_heads = grad_heads.astype(BF)
    for h in range(heads):
        q = qkv_ref[:, h * HD : (h + 1) * HD]
        k = qkv_ref[:, group + h * HD : group + (h + 1) * HD]
        v = qkv_ref[:, 2 * group + h * HD : 2 * group + (h + 1) * HD]
        g = grad_heads[:, h * HD : (h + 1) * HD]
        probs = jnp.exp(mm_nt(q, k) * scale - lse_ref[:, h : h + 1])
        grad_p = mm_nt(g, v)
        dots = jnp.sum(probs * grad_p, axis=-1, keepdims=True)
        grad_s = (probs * (grad_p - dots) * scale).astype(BF)
        gqkv_ref[:, h * HD : (h + 1) * HD] = mm(grad_s, k).astype(BF)
        gqkv_ref[:, group + h * HD : group + (h + 1) * HD] = mm_tn(grad_s, q).astype(BF)
        gqkv_ref[:, 2 * group + h * HD : 2 * group + (h + 1) * HD] = mm_tn(
            probs.astype(BF), g
        ).astype(BF)
    parts, rows, width = part_ref.shape
    part_ref[...] = mm_nt(gqkv_ref[...], w_ref[...]).reshape(parts, rows, width)
    sums_ref[...] = jnp.zeros(sums_ref.shape, F32)
    for j in range(parts):
        dy = part_ref[j]
        hat = hat_ref[j * rows : (j + 1) * rows, :].astype(F32)
        sums_ref[0:1, :] += jnp.sum(dy * hat, axis=0, keepdims=True)
        sums_ref[1:2, :] += jnp.sum(dy, axis=0, keepdims=True)
        part_ref[j] = res_ref[j] + norm_back(hat, stat_ref[j][:, 5:6], gains_ref[0:1, :], dy)
    spread_parts(me_ref[1], part_ref, keep_ref, send)


def spread_parts(me, part_ref, own_ref, send):
    own_ref[...] = part_ref[me]
    for d in range(1, part_ref.shape[0]):
        send[d - 1][...] = part_ref[me ^ d].astype(BF)


def split_pairs(me, temp_ref, keep_ref, send_ref, rows):
    odd = me & 1
    for q in range(keep_ref.shape[0]):
        keep_ref[q, :rows, :] = temp_ref[2 * q + odd]
        send_ref[q, :rows, :] = temp_ref[2 * q + 1 - odd].astype(BF)


def weight_grad_body(me_ref, a_ref, gqkv_ref, one_ref, two_ref, keep_ref, send_ref, temp_ref, line_ref):
    count, rows, width = temp_ref.shape
    temp_ref[...] = mm_tn(a_ref[...], gqkv_ref[...]).reshape(count, rows, width)
    split_pairs(me_ref[0], temp_ref, keep_ref, send_ref, rows)
    line_ref[...] = jnp.zeros(line_ref.shape, F32)
    for f in range(count):
        for k in range(4):
            source = one_ref if k < 2 else two_ref
            line_ref[f, 0:1, k * rows : (k + 1) * rows] = source[
                k % 2 : k % 2 + 1, f * rows : (f + 1) * rows
            ]
    odd = me_ref[0] & 1
    for q in range(keep_ref.shape[0]):
        keep_ref[q, rows:, :] = line_ref[2 * q + odd]
        send_ref[q, rows:, :] = line_ref[2 * q + 1 - odd].astype(BF)


def proj_grad_body(count, me_ref, mix_ref, *refs):
    heads = refs[:count]
    keep_ref, send_ref, full_ref, temp_ref = refs[count:]
    width = heads[0].shape[1]
    for d in range(count):
        start = pl.multiple_of((me_ref[1] ^ d) * width, width)
        full_ref[pl.ds(start, width), :] = mm_tn(heads[d][...], mix_ref[...])
    temp_ref[...] = full_ref[...].reshape(temp_ref.shape)
    split_pairs(me_ref[0], temp_ref, keep_ref, send_ref, temp_ref.shape[1])


def pair_sum_body(me_ref, keep_ref, got_ref, *out_refs):
    pair = me_ref[0] >> 1
    for k, ref in enumerate(out_refs):
        ref[...] = (keep_ref[pair ^ k] + got_ref[pair ^ k].astype(F32)).astype(BF)


def total_of(refs):
    total = refs[0][...].astype(F32)
    for ref in refs[1:]:
        total = total + ref[...].astype(F32)
    return total


def last_sum_body(blocks, rows, count, me_ref, *refs):
    total, proj = total_of(refs[:count]), total_of(refs[count : 2 * count])
    sends, out_ref = refs[2 * count : -1], refs[-1]
    each, cols = rows // blocks, total.shape[1]
    out_ref[...] = jnp.zeros(out_ref.shape, BF)
    for s in range(blocks):
        out_ref[s, :each, :cols] = total[s * each : (s + 1) * each, :].astype(BF)
        out_ref[s, :each, cols:] = proj[s * each : (s + 1) * each, :].astype(BF)
        for k in range(4):
            start = k * rows + s * each
            out_ref[s, each : each + 1, k * each : (k + 1) * each] = total[
                rows : rows + 1, start : start + each
            ].astype(BF)
    for d, ref in enumerate(sends):
        ref[...] = out_ref[me_ref[1] ^ d]


def last_body(each, group, me_ref, *refs):
    out_ref, proj_ref, line_ref, parts_ref = refs[-4:]
    blocks = parts_ref.shape[0]
    for d in range(blocks):
        parts_ref[me_ref[1] ^ d] = refs[d][...]
    width = blocks * group
    line = jnp.zeros(line_ref.shape, F32)
    proj = jnp.zeros(proj_ref.shape, F32)
    for s in range(blocks):
        part = parts_ref[s].astype(F32)
        proj = proj + part[:each, 3 * group :]
        for p in range(3):
            start = p * width + s * group
            out_ref[:, start : start + group] = part[:each, p * group : (p + 1) * group]
        line = line + part[each : each + 1, : line_ref.shape[1]]
    line_ref[...] = line
    proj_ref[...] = proj


def project_body(count, me_ref, pos_ref, hat_ref, stat_ref, x_ref, gains_ref, proj_ref, *refs):
    heads = refs[:count]
    res_ref, own_ref = refs[count : count + 2]
    out_refs = refs[count + 2 : -2]
    acc_ref, ffn_ref = refs[-2:]
    rows = x_ref.shape[0]
    group = heads[0].shape[1]
    for d in range(count):
        start = pl.multiple_of((me_ref[1] ^ d) * group, group)
        piece = mm(heads[d][...], proj_ref[pl.ds(start, group), :])
        acc_ref[...] = piece if d == 0 else acc_ref[...] + piece
    for j in range(count):
        stat = stat_ref[j]
        x = hat_ref[j * rows : (j + 1) * rows, :].astype(F32) / stat[:, 5:6] + stat[:, 4:5]
        x = jnp.where(me_ref[1] == j, x_ref[...], x)
        res_ref[j] = x + acc_ref[j * rows : (j + 1) * rows, :]
        hat, _ = norm_parts(res_ref[j])
        ffn_ref[j * rows : (j + 1) * rows, :] = (
            hat * gains_ref[2:3, :] + gains_ref[3:4, :]
        ).astype(BF)
    own_ref[...] = res_ref[me_ref[1]]
    for d, out_ref in enumerate(out_refs):
        pick = one_hot(pos_ref[pl.ds(me_ref[0] ^ d, 1), :], out_ref.shape[0])
        out_ref[...] = mm(pick, ffn_ref[...]).astype(BF)


def combine_grad_body(experts, me_ref, pos_ref, res_ref, cot_ref, gains_ref, proj_ref, *refs):
    back = refs[:experts]
    dx_ref, mix_ref, sums_ref, keep_ref = refs[experts : experts + 4]
    send = refs[experts + 4 : -1]
    part_ref = refs[-1]
    slots = back[0].shape[0]
    parts, rows, width = part_ref.shape
    for d in range(experts):
        pick = one_hot(pos_ref[pl.ds(me_ref[0] ^ d, 1), :], slots)
        piece = mm_tn(pick, back[d][...]).reshape(parts, rows, width)
        part_ref[...] = piece if d == 0 else part_ref[...] + piece
    sums_ref[...] = jnp.zeros(sums_ref.shape, F32)
    for j in range(parts):
        dy = part_ref[j]
        hat, scale = norm_parts(res_ref[j])
        sums_ref[0:1, :] += jnp.sum(dy * hat, axis=0, keepdims=True)
        sums_ref[1:2, :] += jnp.sum(dy, axis=0, keepdims=True)
        dx = norm_back(hat, scale, gains_ref[2:3, :], dy)
        dx = dx + jnp.where(me_ref[1] == j, cot_ref[...], 0.0)
        dx_ref[j] = dx
        mix_ref[j * rows : (j + 1) * rows, :] = dx.astype(BF)
    group = keep_ref.shape[1]
    for d in range(parts):
        start = pl.multiple_of((me_ref[1] ^ d) * group, group)
        piece = mm_nt(mix_ref[...], proj_ref[pl.ds(start, group), :])
        if d == 0:
            keep_ref[...] = piece
        else:
            send[d - 1][...] = piece.astype(BF)


def combine_out_body(experts, me_ref, pos_ref, gate_ref, back_ref, res_ref, own_ref, *refs):
    send, part_ref = refs[:-1], refs[-1]
    slots = back_ref.shape[1]
    parts, rows, width = part_ref.shape
    part_ref[...] = jnp.zeros(part_ref.shape, F32)

    def step(e, carry):
        chosen = selection(pos_ref[pl.ds(e, 1), :], slots)
        gate = jnp.where(chosen, gate_ref[pl.ds(e, 1), :], 0.0)
        high = gate.astype(BF)
        low = (gate - high.astype(F32)).astype(BF)
        piece = mm_tn(high, back_ref[e]) + mm_tn(low, back_ref[e])
        part_ref[...] += piece.reshape(parts, rows, width)
        return carry

    lax.fori_loop(0, experts, step, 0)
    spread_parts(me_ref[1], part_ref, own_ref, send)
    own_ref[...] += res_ref[...]


def hidden_grad_body(per, me_ref, g_ref, down_ref, *out_refs):
    rows = g_ref.shape[1]
    for g, out_ref in enumerate(out_refs):
        for i in range(per):
            out_ref[i * rows : (i + 1) * rows, :] = mm(
                g_ref[me_ref[0] ^ (g * per + i)], down_ref[...]
            )


def expert_body(count, *refs):
    rows_refs = refs[:count]
    gh_ref, up_ref = refs[count : count + 2]
    gr_refs = refs[count + 2 : 2 * count + 2]
    hid_ref, gp_ref, pre_ref = refs[2 * count + 2 :]
    rows = rows_refs[0].shape[0]
    for i in range(count):
        pre_ref[i * rows : (i + 1) * rows, :] = mm(rows_refs[i][...], up_ref[...])
    tile = 32

    def step(j, carry):
        at = pl.ds(pl.multiple_of(j * tile, tile), tile)
        u = pre_ref[at, :]
        sq = u * u
        t = jnp.tanh(C0 * (u + C1 * (sq * u)))
        half = 0.5 * (1.0 + t)
        hid_ref[at, :] = (u * half).astype(BF)
        slope = half + 0.5 * u * (1.0 - t * t) * (C0 * (1.0 + 3.0 * C1 * sq))
        gp_ref[at, :] = (gh_ref[at, :] * slope).astype(BF)
        return carry

    lax.fori_loop(0, count * rows // tile, step, 0)
    for i in range(count):
        gr_refs[i][...] = mm_nt(gp_ref[i * rows : (i + 1) * rows, :], up_ref[...]).astype(BF)


def expert_out_body(per, me_ref, down_ref, *refs):
    hids, out_ref = refs[:-1], refs[-1]
    rows = out_ref.shape[1]
    for g, hid_ref in enumerate(hids):
        for i in range(per):
            out_ref[me_ref[0] ^ (g * per + i)] = mm_nt(
                hid_ref[i * rows : (i + 1) * rows, :], down_ref[...]
            ).astype(BF)


def grad_up_body(count, *refs):
    lefts, rights, out_ref, temp_ref = refs[: -2 - count], refs[-2 - count : -2], refs[-2], refs[-1]
    rows = lefts[0].shape[0]
    per = len(lefts) // count
    for g in range(count):
        for i in range(per):
            temp_ref[i * rows : (i + 1) * rows, :] = lefts[g * per + i][...]
        piece = mm_tn(temp_ref[...], rights[g][...])
        out_ref[0] = piece if g == 0 else out_ref[0] + piece


def grad_down_body(count, me_ref, left_ref, *refs):
    rights, out_ref, temp_ref = refs[:count], refs[count], refs[count + 1]
    rows = left_ref.shape[1]
    per = left_ref.shape[0] // count
    for g in range(count):
        for i in range(per):
            temp_ref[i * rows : (i + 1) * rows, :] = left_ref[me_ref[0] ^ (g * per + i)]
        piece = mm_tn(temp_ref[...], rights[g][...])
        out_ref[0] = piece if g == 0 else out_ref[0] + piece


def local(
    inputs,
    qkv_weight,
    proj_weight,
    first_gain,
    first_shift,
    second_gain,
    second_shift,
    expert_up,
    expert_down,
    gate_logits,
    routes,
    cotangent,
):
    tok, width = inputs.shape
    ns = lax.axis_size("seq")
    nf = lax.axis_size("fsdp")
    group = width // ns
    heads = group // HD
    length = tok * ns
    slots = ns * (4 * tok // nf)
    wrows = qkv_weight.shape[0]
    cols = 3 * group
    hidden = expert_up.shape[2]
    me = jnp.stack([lax.axis_index("fsdp"), lax.axis_index("seq")]).astype(jnp.int32)
    groups = 4
    per = nf // groups
    bf_block = ((tok, width), BF)

    by_group = qkv_weight.reshape(wrows, 3, ns, group).transpose(2, 0, 1, 3).reshape(ns, wrows, cols)
    packed = jnp.concatenate(
        [by_group, jnp.broadcast_to(proj_weight[None], (ns, wrows, width))], axis=2
    )
    gain_row = jnp.concatenate([first_gain, first_shift, second_gain, second_shift])
    gain_row = jnp.pad(gain_row, (0, cols + width - gain_row.shape[0]))
    packed = jnp.concatenate(
        [packed, jnp.broadcast_to(gain_row[None, None, :], (ns, 1, cols + width))], axis=1
    )
    packed = swap(packed, "seq")
    info = jnp.concatenate([routes.astype(F32), gate_logits], axis=1)
    info = jnp.pad(info, ((0, 0), (0, tok - info.shape[1])))
    hat_own, cot_pack = kernel_call(
        prepare_body, [bf_block, ((tok + 2 * INFO, width), BF)], (inputs, cotangent, info)
    )
    cot_blocks = exchange([cot_pack] * ns, "seq", ns)
    first = lax.all_gather(packed[:, :, :cols], "fsdp", axis=0, tiled=True)
    hat_own, proj_rows, me_late, first = lax.optimization_barrier(
        (hat_own, packed[:, :wrows, cols:].reshape(ns * wrows, width), me, first)
    )
    hat_blocks = exchange([hat_own] * ns, "seq", ns)
    qkv_w = first[:, :wrows].reshape(width, cols)
    gains = (
        first[:, wrows, : 4 * wrows]
        .reshape(nf * ns, 4, wrows)
        .transpose(1, 0, 2)
        .reshape(4, width)
        .astype(F32)
    )
    proj = swap(jnp.broadcast_to(proj_rows[None], (nf, ns * wrows, width)), "fsdp")
    proj = proj.reshape(width, width)

    pos, gate, stats = kernel_call(
        functools.partial(table_body, nf),
        [((nf, length), F32), ((nf, length), F32), ((ns, tok, tok), F32)],
        (me_late, *cot_blocks),
        smem=1,
        scratch=[pltpu.VMEM((ns, INFO, tok), F32)],
    )
    (grad_sent,) = kernel_call(
        functools.partial(dispatch_grad_body, nf, ns),
        [((nf, slots, width), BF)],
        (me, pos, gate, *cot_blocks),
        smem=1,
        scratch=[pltpu.VMEM((length, width), BF)],
    )
    grad_in = swap(grad_sent, "fsdp")
    up, down = expert_up[0], expert_down[0]

    hat, attn_in, qkv, heads_s, lse = kernel_call(
        functools.partial(attention_forward_body, heads),
        [
            ((length, width), BF),
            ((length, width), BF),
            ((length, cols), BF),
            ((length, group), BF),
            ((length, 128), F32),
        ],
        (me, gains, qkv_w, *hat_blocks),
        smem=1,
    )
    heads_all = exchange([heads_s] * ns, "seq", ns)
    grad_hidden = kernel_call(
        functools.partial(hidden_grad_body, per),
        [((per * slots, hidden), F32)] * groups,
        (me, grad_in, down),
        smem=1,
    )
    res_all, residual, *sent = kernel_call(
        functools.partial(project_body, ns),
        [((ns, tok, width), F32), ((tok, width), F32)] + [((slots, width), BF)] * nf,
        (me, pos, hat, stats, inputs, gains, proj, *heads_all),
        smem=1,
        scratch=[pltpu.VMEM((length, width), F32), pltpu.VMEM((length, width), BF)],
    )
    rows_in = exchange(sent, "fsdp", nf)
    grad_rows, hid, grad_pre = [], [], []
    for g in range(groups):
        res = kernel_call(
            functools.partial(expert_body, per),
            [((slots, width), BF)] * per + [((per * slots, hidden), BF)] * 2,
            (*rows_in[g * per : (g + 1) * per], grad_hidden[g], up),
            scratch=[pltpu.VMEM((per * slots, hidden), F32)],
        )
        grad_rows += res[:per]
        hid.append(res[per])
        grad_pre.append(res[per + 1])
    grad_back = exchange(grad_rows, "fsdp", nf)
    (expert_out,) = kernel_call(
        functools.partial(expert_out_body, per),
        [((nf, slots, width), BF)],
        (me, down, *hid),
        smem=1,
    )
    temp = [pltpu.VMEM((per * slots, width), BF)]
    (grad_up,) = kernel_call(
        functools.partial(grad_up_body, groups),
        [((1, width, hidden), F32)],
        (*rows_in, *grad_pre),
        scratch=temp,
    )
    (grad_down,) = kernel_call(
        functools.partial(grad_down_body, groups),
        [((1, width, hidden), F32)],
        (me, grad_in, *hid),
        smem=1,
        scratch=temp,
    )

    image = [pltpu.VMEM((ns, tok, width), F32)]
    share = [((tok, width), F32)] + [bf_block] * (ns - 1)
    grad_res, mix, sums_two, gh_own, *gh_sent = kernel_call(
        functools.partial(combine_grad_body, nf),
        [
            ((ns, tok, width), F32),
            ((length, width), BF),
            ((2, width), F32),
            ((length, group), F32),
        ]
        + [((length, group), BF)] * (ns - 1),
        (me, pos, res_all, cotangent, gains, proj, *grad_back),
        smem=1,
        scratch=image,
    )
    out_back = swap(after(expert_out, gh_own), "fsdp")
    gh_got = exchange([None] + gh_sent, "seq", ns)[1:]
    grad_qkv, sums_one, grad_own, *grad_share = kernel_call(
        functools.partial(attention_backward_body, heads),
        [((length, cols), BF), ((2, width), F32)] + share,
        (me, gh_own, *gh_got, qkv, lse, qkv_w, hat, stats, gains, grad_res),
        smem=1,
        scratch=image,
    )
    grad_inputs = grad_own
    for piece in exchange([None] + grad_share, "seq", ns)[1:]:
        grad_inputs = grad_inputs + piece.astype(F32)
    wide = ns * wrows
    half = nf // 2

    def over_chips(keep, sent):
        got = lax.ppermute(sent, "fsdp", [(i, i ^ 1) for i in range(nf)])
        both = kernel_call(pair_sum_body, [(keep.shape[1:], BF)] * half, (me, keep, got), smem=1)
        return exchange(both, "fsdp", nf, stride=2)

    keep_p, send_p = kernel_call(
        functools.partial(proj_grad_body, ns),
        [((half, wide, width), F32), ((half, wide, width), BF)],
        (me, mix, *heads_all),
        smem=1,
        scratch=[pltpu.VMEM((width, width), F32), pltpu.VMEM((nf, wide, width), F32)],
    )
    parts_p = over_chips(keep_p, send_p)
    keep_q, send_q = kernel_call(
        weight_grad_body,
        [((half, wide + 8, cols), F32), ((half, wide + 8, cols), BF)],
        (me, attn_in, grad_qkv, sums_one, sums_two),
        smem=1,
        scratch=[pltpu.VMEM((nf, wide, cols), F32), pltpu.VMEM((nf, 8, cols), F32)],
    )
    parts_q = over_chips(keep_q, send_q)
    last = kernel_call(
        functools.partial(last_sum_body, ns, wide, half),
        [((wrows + 8, cols + width), BF)] * ns,
        (me, *parts_q, *parts_p),
        smem=1,
        scratch=[pltpu.VMEM((ns, wrows + 8, cols + width), BF)],
    )
    last = exchange(last, "seq", ns)
    grad_qkv_weight, grad_proj, line = kernel_call(
        functools.partial(last_body, wrows, group),
        [((wrows, 3 * width), F32), ((wrows, width), F32), ((1, 128), F32)],
        (me, *last),
        smem=1,
        scratch=[pltpu.VMEM((ns, wrows + 8, cols + width), BF)],
    )
    tiny = line[0, : 4 * wrows].reshape(4, wrows)
    output, *out_share = kernel_call(
        functools.partial(combine_out_body, nf),
        share,
        (me, pos, gate, out_back, residual),
        smem=1,
        scratch=image,
    )
    for piece in exchange([None] + out_share, "seq", ns)[1:]:
        output = output + piece.astype(F32)

    return (
        output,
        grad_inputs,
        grad_qkv_weight,
        grad_proj,
        tiny[0],
        tiny[1],
        tiny[2],
        tiny[3],
        grad_up,
        grad_down,
    )


def solution(mesh):
    both = ("fsdp", "seq")
    rows, line, expert = P(both, None), P(both), P("fsdp", None, "seq")
    in_specs = (rows, rows, rows, line, line, line, line, expert, expert, rows, rows, rows)
    out_specs = (rows, rows, rows, rows, line, line, line, line, expert, expert)
    return jax.shard_map(local, mesh=mesh, in_specs=in_specs, out_specs=out_specs, check_vma=False)
```

profile of v0, /device:TPU:0, one launch (start us, length us, event | category | flops | bytes accessed | tf_op | source)
XLA Modules:
  0.0 333.1 jit_solution(905354205637827519)
XLA Ops:
  4.4 6.3 %all-to-all-start = ((bf16[4,25,1344]{2,1,0:T(8,128)(2,1)}), bf16[4,25,1344]{2,1,0:T(8,128)(2,1)S(1)}, u32[]{:S(2)}, u32[]{:S(2)}) async-start(bf16[4,25,1344]{2,1,0:T(8,128)(2,1)} %fusion), calls=%async_computation | async-start | bytes 720896 | tf_op jit(solution)/shard_map/all_to_all | solution.py:51
  14.2 7.5 %all-to-all-done = bf16[4,25,1344]{2,1,0:T(8,128)(2,1)S(1)} async-done(((bf16[4,25,1344]{2,1,0:T(8,128)(2,1)}), bf16[4,25,1344]{2,1,0:T(8,128)(2,1)S(1)}, u32[]{:S(2)}, u32[]{:S(2)}) %all-to-all-start) | async-done | bytes 268832 | tf_op jit(solution)/shard_map/all_to_all | solution.py:51
  21.8 12.9 %all_gather.3 = bf16[32,25,576]{2,1,0:T(8,128)(2,1)} all-gather(bf16[4,25,576]{2,1,0:T(8,128)(2,1)S(1)} %slice.42), channel_id=1, replica_groups=mesh['fsdp'=8,'seq'=4] {'fsdp'}, dimensions={0}, use_global_device_ids=true | all-gather | bytes 1036800 | tf_op jit(solution)/shard_map/all_gather | solution.py:503
  44.0 5.9 %collective-permute-done.2.refs_3_ = bf16[144,768]{1,0:T(8,128)(2,1)S(1)} collective-permute-done((bf16[144,768]{1,0:T(8,128)(2,1)S(1)}, bf16[144,768]{1,0:T(8,128)(2,1)S(1)}, u32[]{:S(2)}, u32[]{:S(2)}) %collective-permute-start.2) | collective-permute-done | bytes 221216 | tf_op jit(solution)/shard_map/ppermute | solution.py:46
  49.8 10.7 %collective-permute-done.1.refs_2_ = bf16[144,768]{1,0:T(8,128)(2,1)S(1)} collective-permute-done((bf16[144,768]{1,0:T(8,128)(2,1)S(1)}, bf16[144,768]{1,0:T(8,128)(2,1)S(1)}, u32[]{:S(2)}, u32[]{:S(2)}) %collective-permute-start.1) | collective-permute-done | bytes 221216 | tf_op jit(solution)/shard_map/ppermute | solution.py:46
  64.0 6.1 %shard_map.199 = bf16[8,256,768]{2,1,0:T(8,128)(2,1)} custom-call(s32[2]{0:T(128)} %pad_add_fusion.me_ref.refs_0_, f32[8,512]{1,0:T(8,128)} %get-tuple-element.94.pos_ref, f32[8,512]{1,0:T(8,128)} %get-tuple-element.95.gate_ref, bf16[144,768]{1,0:T(8,128)(2,1)} %get-tuple-element.93.refs_0_, bf16[144,768]{1,0:T(8,128)(2,1)} %copy-done.10, ...), custom_call_target="tpu_custom_call" | custom-call | tf_op jit(solution)/shard_map/pallas_call | solution.py:34
  85.4 8.4 %collective-permute-done.4.refs_2_ = bf16[128,768]{1,0:T(8,128)(2,1)} collective-permute-done((bf16[128,768]{1,0:T(8,128)(2,1)S(1)}, bf16[128,768]{1,0:T(8,128)(2,1)}, u32[]{:S(2)}, u32[]{:S(2)}) %collective-permute-start.4) | collective-permute-done | bytes 196640 | tf_op jit(solution)/shard_map/ppermute | solution.py:46
  103.3 6.9 %collective-permute-done.8.refs_3_ = bf16[512,192]{1,0:T(8,128)(2,1)S(1)} collective-permute-done((bf16[512,192]{1,0:T(8,128)(2,1)}, bf16[512,192]{1,0:T(8,128)(2,1)S(1)}, u32[]{:S(2)}, u32[]{:S(2)}) %collective-permute-start.8) | collective-permute-done | bytes 196640 | tf_op jit(solution)/shard_map/ppermute | solution.py:46
  110.2 12.6 %collective-permute-done.7.refs_2_ = bf16[512,192]{1,0:T(8,128)(2,1)} collective-permute-done((bf16[512,192]{1,0:T(8,128)(2,1)}, bf16[512,192]{1,0:T(8,128)(2,1)}, u32[]{:S(2)}, u32[]{:S(2)}) %collective-permute-start.7) | collective-permute-done | bytes 196640 | tf_op jit(solution)/shard_map/ppermute | solution.py:46
  122.7 6.4 %shard_map.198 = (f32[4,128,768]{2,1,0:T(8,128)}, f32[128,768]{1,0:T(8,128)}, bf16[256,768]{1,0:T(8,128)(2,1)}, bf16[256,768]{1,0:T(8,128)(2,1)}, bf16[256,768]{...) custom-call(s32[2]{0:T(128)} %pad_add_fusion.me_ref.refs_0_, ...), custom_call_target="tpu_custom_call" | custom-call | tf_op jit(solution)/shard_map/pallas_call | solution.py:34
  136.3 6.1 %shard_map.200 = (f32[512,768]{1,0:T(8,128)}, f32[512,768]{1,0:T(8,128)}, f32[512,768]{1,0:T(8,128)}, f32[512,768]{1,0:T(8,128)}) custom-call(s32[2]{0:T(128)} %pad_add_fusion.me_ref.refs_0_, bf16[8,256,768]{2,1,0:T(8,128)(2,1)} %copy-done, bf16[768,768]{1,0:T(8,128)(2,1)} %bitcast.27), custom_call_target="tpu_custom_call" | custom-call | tf_op jit(solution)/shard_map/pallas_call | solution.py:34
  143.1 5.9 %shard_map.201 = (bf16[256,768]{1,0:T(8,128)(2,1)}, bf16[256,768]{1,0:T(8,128)(2,1)}, bf16[512,768]{1,0:T(8,128)(2,1)}, bf16[512,768]{1,0:T(8,128)(2,1)}) custom-call(bf16[256,768]{1,0:T(8,128)(2,1)} %get-tuple-element.102.refs_0_, bf16[256,768]{1,0:T(8,128)(2,1)} %copy-done.3, f32[512,768]{1,0:T(8,128)} %get-tuple-element.104.refs_2_, bf16[768,768]{1,0:T(8,128)(2,1)} %bitcast.19), custom_call_target="tpu_custom_call" | custom-call | tf_op jit(solution)/shard_map/pallas_call | solution.py:34
  150.7 5.9 %shard_map.204 = (bf16[256,768]{1,0:T(8,128)(2,1)}, bf16[256,768]{1,0:T(8,128)(2,1)}, bf16[512,768]{1,0:T(8,128)(2,1)}, bf16[512,768]{1,0:T(8,128)(2,1)}) custom-call(bf16[256,768]{1,0:T(8,128)(2,1)} %collective-permute-done.14.refs_0_.refs_6_, bf16[256,768]{1,0:T(8,128)(2,1)} %collective-permute-done.15.refs_1_.refs_7_, ...), custom_call_target="tpu_custom_call" | custom-call | tf_op jit(solution)/shard_map/pallas_call | solution.py:34
  161.0 6.5 %collective-permute-done.13.refs_1_.refs_5_ = bf16[256,768]{1,0:T(8,128)(2,1)S(1)} collective-permute-done((bf16[256,768]{1,0:T(8,128)(2,1)}, bf16[256,768]{1,0:T(8,128)(2,1)S(1)}, u32[]{:S(2)}, u32[]{:S(2)}) %collective-permute-start.13) | collective-permute-done | bytes 393248 | tf_op jit(solution)/shard_map/ppermute | solution.py:46
  184.4 6.5 %shard_map.205 = bf16[8,256,768]{2,1,0:T(8,128)(2,1)} custom-call(s32[2]{0:T(128)} %pad_add_fusion.me_ref.refs_0_, bf16[768,768]{1,0:T(8,128)(2,1)} %bitcast.28, bf16[512,768]{1,0:T(8,128)(2,1)} %get-tuple-element.105.refs_0_, bf16[512,768]{1,0:T(8,128)(2,1)} %get-tuple-element.109.refs_1_, bf16[512,768]{1,0:T(8,128)(2,1)} %get-tuple-element.113.refs_2_, ...), custom_call_target="tpu_custom_call" | custom-call | tf_op jit(solution)/shard_map/pallas_call | solution.py:34
  192.5 8.3 %collective-permute-done.20.refs_5_ = bf16[256,768]{1,0:T(8,128)(2,1)S(1)} collective-permute-done((bf16[256,768]{1,0:T(8,128)(2,1)}, bf16[256,768]{1,0:T(8,128)(2,1)S(1)}, u32[]{:S(2)}, u32[]{:S(2)}) %collective-permute-start.20) | collective-permute-done | bytes 393248 | tf_op jit(solution)/shard_map/ppermute | solution.py:46
  202.9 7.6 %shard_map.206 = (f32[4,128,768]{2,1,0:T(8,128)}, bf16[512,768]{1,0:T(8,128)(2,1)}, f32[2,768]{1,0:T(2,128)}, f32[512,192]{1,0:T(8,128)}, bf16[512,192]{1,0:T(8,...) custom-call(s32[2]{0:T(128)} %pad_add_fusion.me_ref.refs_0_, f32[8,512]{1,0:T(8,128)} %get-tuple-element.94.pos_ref, ...), custom_call_target="tpu_custom_call" | custom-call | tf_op jit(solution)/shard_map/pallas_call | solution.py:34
  222.8 9.1 %collective-permute-done.26.refs_2_ = bf16[512,192]{1,0:T(8,128)(2,1)S(1)} collective-permute-done((bf16[512,192]{1,0:T(8,128)(2,1)}, bf16[512,192]{1,0:T(8,128)(2,1)S(1)}, u32[]{:S(2)}, u32[]{:S(2)}) %collective-permute-start.26) | collective-permute-done | bytes 196640 | tf_op jit(solution)/shard_map/ppermute | solution.py:46
  231.9 8.1 %collective-permute-done.27.refs_3_ = bf16[512,192]{1,0:T(8,128)(2,1)} collective-permute-done((bf16[512,192]{1,0:T(8,128)(2,1)}, bf16[512,192]{1,0:T(8,128)(2,1)}, u32[]{:S(2)}, u32[]{:S(2)}) %collective-permute-start.27) | collective-permute-done | bytes 196640 | tf_op jit(solution)/shard_map/ppermute | solution.py:46
  240.1 8.0 %shard_map.208 = (bf16[512,576]{1,0:T(8,128)(2,1)}, f32[2,768]{1,0:T(2,128)}, f32[128,768]{1,0:T(8,128)}, bf16[128,768]{1,0:T(8,128)(2,1)}, bf16[128,768]{1,0:T(8,128)(2,1)}, /*index=5*/bf16[128,768]{1,0:T(8,128)(2,1)}) custom-call(s32[2]{0:T(128)} %pad_add_fusion.me_ref.refs_0_, f32[512,192]{1,0:T(8,128)} %get-tuple-element.127.refs_1_, ...), custom_call_target="tpu_custom_call" | custom-call | tf_op jit(solution)/shard_map/pallas_call | solution.py:34
  272.1 6.9 %shard_map.216 = f32[1,768,768]{2,1,0:T(8,128)} custom-call(s32[2]{0:T(128)} %pad_add_fusion.me_ref.refs_0_, bf16[8,256,768]{2,1,0:T(8,128)(2,1)} %copy-done, bf16[512,768]{1,0:T(8,128)(2,1)} %get-tuple-element.105.refs_0_, bf16[512,768]{1,0:T(8,128)(2,1)} %get-tuple-element.109.refs_1_, bf16[512,768]{1,0:T(8,128)(2,1)} %get-tuple-element.113.refs_2_, ...), custom_call_target="tpu_custom_call" | custom-call | tf_op jit(solution)/shard_map/pallas_call | solution.py:34
  279.0 6.9 %shard_map.215 = f32[1,768,768]{2,1,0:T(8,128)} custom-call(bf16[256,768]{1,0:T(8,128)(2,1)} %get-tuple-element.102.refs_0_, bf16[256,768]{1,0:T(8,128)(2,1)} %copy-done.3, bf16[256,768]{1,0:T(8,128)(2,1)} %collective-permute-done.10.refs_0_.refs_2_, bf16[256,768]{1,0:T(8,128)(2,1)} %copy-done.5, bf16[256,768]{1,0:T(8,128)(2,1)} %collective-permute-done.12.refs_0_.refs_4_, ...), custom_call_target="tpu_custom_call" | custom-call | tf_op jit(solution)/shard_map/pallas_call | solution.py:34
  304.0 8.1 %shard_map.207 = (f32[128,768]{1,0:T(8,128)}, bf16[128,768]{1,0:T(8,128)(2,1)}, bf16[128,768]{1,0:T(8,128)(2,1)}, bf16[128,768]{1,0:T(8,128)(2,1)}) custom-call(s32[2]{0:T(128)} %pad_add_fusion.me_ref.refs_0_, f32[8,512]{1,0:T(8,128)} %get-tuple-element.94.pos_ref, f32[8,512]{1,0:T(8,128)} %get-tuple-element.95.gate_ref, bf16[8,256,768]{2,1,0:T(8,128)(2,1)} %copy-done.1, ...), custom_call_target="tpu_custom_call" | custom-call | tf_op jit(solution)/shard_map/pallas_call | solution.py:34
  321.1 9.9 %collective-permute-done.24 = bf16[128,768]{1,0:T(8,128)(2,1)S(1)} collective-permute-done((bf16[128,768]{1,0:T(8,128)(2,1)}, bf16[128,768]{1,0:T(8,128)(2,1)S(1)}, u32[]{:S(2)}, u32[]{:S(2)}) %collective-permute-start.24) | collective-permute-done | bytes 196640 | tf_op jit(solution)/shard_map/ppermute | solution.py:46
  (170 shorter events, 144.4 us)
Async XLA Ops:
  35.9 34.2 %all-to-all-start.1 = ((bf16[8,96,768]{2,1,0:T(8,128)(2,1)}), bf16[8,96,768]{2,1,0:T(8,128)(2,1)S(1)}, u32[]{:S(2)}, u32[]{:S(2)}) async-start(bf16[8,96,768]{2,1,0:T(8,128)(2,1)} %broadcast_in_dim.8), calls=%async_computation.1 | async-start | bytes 2359296 | tf_op jit(solution)/shard_map/all_to_all | solution.py:51
  41.0 19.5 %collective-permute-start.1 = (bf16[144,768]{1,0:T(8,128)(2,1)S(1)}, bf16[144,768]{1,0:T(8,128)(2,1)S(1)}, u32[]{:S(2)}, u32[]{:S(2)}) collective-permute-start(bf16[144,768]{1,0:T(8,128)(2,1)S(1)} %copy-done.7), channel_id=1, source_target_pairs={{0,2},{1,3},{2,0},{3,1},{4,6},{5,7},{6,4},{7,5},{8,10},{9,11},{10,... | collective-permute-start | bytes 663560 | tf_op jit(solution)/shard_map/ppermute | solution.py:46
  41.0 19.5 %collective-permute-start = (bf16[144,768]{1,0:T(8,128)(2,1)S(1)}, bf16[144,768]{1,0:T(8,128)(2,1)S(1)}, u32[]{:S(2)}, u32[]{:S(2)}) collective-permute-start(bf16[144,768]{1,0:T(8,128)(2,1)S(1)} %copy-done.7), channel_id=1, source_target_pairs={{0,1},{1,0},{2,3},{3,2},{4,5},{5,4},{6,7},{7,6},{8,9},{9,8},{10,11... | collective-permute-start | bytes 663560 | tf_op jit(solution)/shard_map/ppermute | solution.py:46
  71.2 63.5 %all-to-all-start.2 = ((bf16[8,256,768]{2,1,0:T(8,128)(2,1)}), bf16[8,256,768]{2,1,0:T(8,128)(2,1)S(1)}, u32[]{:S(2)}, u32[]{:S(2)}) async-start(bf16[8,256,768]{2,1,0:T(8,128)(2,1)} %shard_map.199), calls=%async_computation.2 | async-start | bytes 6291456 | tf_op jit(solution)/shard_map/all_to_all | solution.py:51
  101.2 21.5 %collective-permute-start.7 = (bf16[512,192]{1,0:T(8,128)(2,1)}, bf16[512,192]{1,0:T(8,128)(2,1)}, u32[]{:S(2)}, u32[]{:S(2)}) collective-permute-start(bf16[512,192]{1,0:T(8,128)(2,1)} %get-tuple-element.101.refs_0_), channel_id=1, source_target_pairs={{0,2},{1,3},{2,0},{3,1},{4,6},{5,7},{6,4},{7,5},{8,10},{9,11},{10,... | collective-permute-start | bytes 589832 | tf_op jit(solution)/shard_map/ppermute | solution.py:46
  101.2 21.5 %collective-permute-start.6 = (bf16[512,192]{1,0:T(8,128)(2,1)}, bf16[512,192]{1,0:T(8,128)(2,1)}, u32[]{:S(2)}, u32[]{:S(2)}) collective-permute-start(bf16[512,192]{1,0:T(8,128)(2,1)} %get-tuple-element.101.refs_0_), channel_id=1, source_target_pairs={{0,1},{1,0},{2,3},{3,2},{4,5},{5,4},{6,7},{7,6},{8,9},{9,8},{10,11... | collective-permute-start | bytes 589832 | tf_op jit(solution)/shard_map/ppermute | solution.py:46
  129.2 19.8 %collective-permute-start.14 = (bf16[256,768]{1,0:T(8,128)(2,1)}, bf16[256,768]{1,0:T(8,128)(2,1)}, u32[]{:S(2)}, u32[]{:S(2)}) collective-permute-start(bf16[256,768]{1,0:T(8,128)(2,1)} %get-tuple-element.114), channel_id=1, source_target_pairs={{0,24},{4,28},{8,16},{12,20},{16,8},{20,12},{24,0},{28,4},{1,25},{... | collective-permute-start | bytes 1179656 | tf_op jit(solution)/shard_map/ppermute | solution.py:46
  131.4 18.5 %collective-permute-start.15 = (bf16[256,768]{1,0:T(8,128)(2,1)}, bf16[256,768]{1,0:T(8,128)(2,1)}, u32[]{:S(2)}, u32[]{:S(2)}) collective-permute-start(bf16[256,768]{1,0:T(8,128)(2,1)} %get-tuple-element.115), channel_id=1, source_target_pairs={{0,28},{4,24},{8,20},{12,16},{16,12},{20,8},{24,4},{28,0},{1,29},{... | collective-permute-start | bytes 1179656 | tf_op jit(solution)/shard_map/ppermute | solution.py:46
  131.9 26.9 %collective-permute-start.12 = (bf16[256,768]{1,0:T(8,128)(2,1)}, bf16[256,768]{1,0:T(8,128)(2,1)}, u32[]{:S(2)}, u32[]{:S(2)}) collective-permute-start(bf16[256,768]{1,0:T(8,128)(2,1)} %get-tuple-element.110), channel_id=1, source_target_pairs={{0,16},{4,20},{8,24},{12,28},{16,0},{20,4},{24,8},{28,12},{1,17},{... | collective-permute-start | bytes 1179656 | tf_op jit(solution)/shard_map/ppermute | solution.py:46
  133.2 41.9 %collective-permute-start.10 = (bf16[256,768]{1,0:T(8,128)(2,1)}, bf16[256,768]{1,0:T(8,128)(2,1)}, u32[]{:S(2)}, u32[]{:S(2)}) collective-permute-start(bf16[256,768]{1,0:T(8,128)(2,1)} %get-tuple-element.106), channel_id=1, source_target_pairs={{0,8},{4,12},{8,0},{12,4},{16,24},{20,28},{24,16},{28,20},{1,9},{5... | collective-permute-start | bytes 1179656 | tf_op jit(solution)/shard_map/ppermute | solution.py:46
  142.4 25.1 %collective-permute-start.13 = (bf16[256,768]{1,0:T(8,128)(2,1)}, bf16[256,768]{1,0:T(8,128)(2,1)S(1)}, u32[]{:S(2)}, u32[]{:S(2)}) collective-permute-start(bf16[256,768]{1,0:T(8,128)(2,1)} %get-tuple-element.111), channel_id=1, source_target_pairs={{0,20},{4,16},{8,28},{12,24},{16,4},{20,0},{24,12},{28,8},{1,21},{... | collective-permute-start | bytes 1179656 | tf_op jit(solution)/shard_map/ppermute | solution.py:46
  149.0 26.6 %collective-permute-start.11 = (bf16[256,768]{1,0:T(8,128)(2,1)S(1)}, bf16[256,768]{1,0:T(8,128)(2,1)S(1)}, u32[]{:S(2)}, u32[]{:S(2)}) collective-permute-start(bf16[256,768]{1,0:T(8,128)(2,1)S(1)} %copy-done.26), channel_id=1, source_target_pairs={{0,12},{4,8},{8,4},{12,0},{16,28},{20,24},{24,20},{28,16},{1,13},{... | collective-permute-start | bytes 1179656 | tf_op jit(solution)/shard_map/ppermute | solution.py:46
  149.9 32.7 %collective-permute-start.16 = (bf16[256,768]{1,0:T(8,128)(2,1)}, bf16[256,768]{1,0:T(8,128)(2,1)S(1)}, u32[]{:S(2)}, u32[]{:S(2)}) collective-permute-start(bf16[256,768]{1,0:T(8,128)(2,1)} %get-tuple-element.120), channel_id=1, source_target_pairs={{0,4},{4,0},{8,12},{12,8},{16,20},{20,16},{24,28},{28,24},{1,5},{5... | collective-permute-start | bytes 1179656 | tf_op jit(solution)/shard_map/ppermute | solution.py:46
  158.8 24.5 %collective-permute-start.21 = (bf16[256,768]{1,0:T(8,128)(2,1)}, bf16[256,768]{1,0:T(8,128)(2,1)S(1)}, u32[]{:S(2)}, u32[]{:S(2)}) collective-permute-start(bf16[256,768]{1,0:T(8,128)(2,1)} %get-tuple-element.125), channel_id=1, source_target_pairs={{0,24},{4,28},{8,16},{12,20},{16,8},{20,12},{24,0},{28,4},{1,25},{... | collective-permute-start | bytes 1179656 | tf_op jit(solution)/shard_map/ppermute | solution.py:46
  167.5 23.4 %collective-permute-start.22 = (bf16[256,768]{1,0:T(8,128)(2,1)}, bf16[256,768]{1,0:T(8,128)(2,1)S(1)}, u32[]{:S(2)}, u32[]{:S(2)}) collective-permute-start(bf16[256,768]{1,0:T(8,128)(2,1)} %get-tuple-element.126), channel_id=1, source_target_pairs={{0,28},{4,24},{8,20},{12,16},{16,12},{20,8},{24,4},{28,0},{1,29},{... | collective-permute-start | bytes 1179656 | tf_op jit(solution)/shard_map/ppermute | solution.py:46
  175.6 25.1 %collective-permute-start.20 = (bf16[256,768]{1,0:T(8,128)(2,1)}, bf16[256,768]{1,0:T(8,128)(2,1)S(1)}, u32[]{:S(2)}, u32[]{:S(2)}) collective-permute-start(bf16[256,768]{1,0:T(8,128)(2,1)} %get-tuple-element.124), channel_id=1, source_target_pairs={{0,20},{4,16},{8,28},{12,24},{16,4},{20,0},{24,12},{28,8},{1,21},{... | collective-permute-start | bytes 1179656 | tf_op jit(solution)/shard_map/ppermute | solution.py:46
  183.3 18.9 %collective-permute-start.18 = (bf16[256,768]{1,0:T(8,128)(2,1)}, bf16[256,768]{1,0:T(8,128)(2,1)S(1)}, u32[]{:S(2)}, u32[]{:S(2)}) collective-permute-start(bf16[256,768]{1,0:T(8,128)(2,1)} %get-tuple-element.122), channel_id=1, source_target_pairs={{0,12},{4,8},{8,4},{12,0},{16,28},{20,24},{24,20},{28,16},{1,13},{... | collective-permute-start | bytes 1179656 | tf_op jit(solution)/shard_map/ppermute | solution.py:46
  210.5 91.9 %all-to-all-start.3 = ((bf16[8,256,768]{2,1,0:T(8,128)(2,1)}), bf16[8,256,768]{2,1,0:T(8,128)(2,1)S(1)}, u32[]{:S(2)}, u32[]{:S(2)}) async-start(bf16[8,256,768]{2,1,0:T(8,128)(2,1)} %shard_map.205), calls=%async_computation.3 | async-start | bytes 6291456 | tf_op jit(solution)/shard_map/all_to_all | solution.py:51
  218.0 33.7 %collective-permute-start.36 = (bf16[4,96,768]{2,1,0:T(8,128)(2,1)}, bf16[4,96,768]{2,1,0:T(8,128)(2,1)}, u32[]{:S(2)}, u32[]{:S(2)}) collective-permute-start(bf16[4,96,768]{2,1,0:T(8,128)(2,1)} %get-tuple-element.156), channel_id=1, source_target_pairs={{0,4},{4,0},{8,12},{12,8},{16,20},{20,16},{24,28},{28,24},{1,5},{5... | collective-permute-start | bytes 1769480 | tf_op jit(solution)/shard_map/ppermute | solution.py:627
  218.4 21.7 %collective-permute-start.27 = (bf16[512,192]{1,0:T(8,128)(2,1)}, bf16[512,192]{1,0:T(8,128)(2,1)}, u32[]{:S(2)}, u32[]{:S(2)}) collective-permute-start(bf16[512,192]{1,0:T(8,128)(2,1)} %get-tuple-element.135), channel_id=1, source_target_pairs={{0,2},{1,3},{2,0},{3,1},{4,6},{5,7},{6,4},{7,5},{8,10},{9,11},{10,... | collective-permute-start | bytes 589832 | tf_op jit(solution)/shard_map/ppermute | solution.py:46
  221.2 18.9 %collective-permute-start.28 = (bf16[512,192]{1,0:T(8,128)(2,1)}, bf16[512,192]{1,0:T(8,128)(2,1)}, u32[]{:S(2)}, u32[]{:S(2)}) collective-permute-start(bf16[512,192]{1,0:T(8,128)(2,1)} %get-tuple-element.136), channel_id=1, source_target_pairs={{0,3},{1,2},{2,1},{3,0},{4,7},{5,6},{6,5},{7,4},{8,11},{9,10},{10,... | collective-permute-start | bytes 589832 | tf_op jit(solution)/shard_map/ppermute | solution.py:46
  261.5 30.2 %collective-permute-start.29 = (bf16[128,768]{1,0:T(8,128)(2,1)}, bf16[128,768]{1,0:T(8,128)(2,1)}, u32[]{:S(2)}, u32[]{:S(2)}) collective-permute-start(bf16[128,768]{1,0:T(8,128)(2,1)} %get-tuple-element.141), channel_id=1, source_target_pairs={{0,1},{1,0},{2,3},{3,2},{4,5},{5,4},{6,7},{7,6},{8,9},{9,8},{10,11... | collective-permute-start | bytes 589832 | tf_op jit(solution)/shard_map/ppermute | solution.py:46
  267.1 26.2 %collective-permute-start.30 = (bf16[128,768]{1,0:T(8,128)(2,1)}, bf16[128,768]{1,0:T(8,128)(2,1)}, u32[]{:S(2)}, u32[]{:S(2)}) collective-permute-start(bf16[128,768]{1,0:T(8,128)(2,1)} %get-tuple-element.142), channel_id=1, source_target_pairs={{0,2},{1,3},{2,0},{3,1},{4,6},{5,7},{6,4},{7,5},{8,10},{9,11},{10,... | collective-permute-start | bytes 589832 | tf_op jit(solution)/shard_map/ppermute | solution.py:46
  267.9 25.4 %collective-permute-start.31 = (bf16[128,768]{1,0:T(8,128)(2,1)}, bf16[128,768]{1,0:T(8,128)(2,1)}, u32[]{:S(2)}, u32[]{:S(2)}) collective-permute-start(bf16[128,768]{1,0:T(8,128)(2,1)} %get-tuple-element.143), channel_id=1, source_target_pairs={{0,3},{1,2},{2,1},{3,0},{4,7},{5,6},{6,5},{7,4},{8,11},{9,10},{10,... | collective-permute-start | bytes 589832 | tf_op jit(solution)/shard_map/ppermute | solution.py:46
  (50 other events, 465.7 us)
where the time goes:
time: 337 us; the launch traced here: 333 us
  Pallas kernels  111 us (33%)
  waiting for transfers between devices  110 us (33%)
  starting transfers between devices  75.8 us (22%)
  local copies, waits for them, and re-layouts  14.9 us (4%)
  blocking collectives  12.9 us (4%)
  other arithmetic  6.9 us (2%)
    pallas_call x22, Pallas kernels, kernel_call(): pl.pallas_call(body, out_shape=[jax.ShapeDtypeStruct(s, d) for s, d in ou...  111 us
    ppermute x41, waiting for transfers between devices, exchange(): lax.ppermute(chunks[d // stride], axis, [(i, i ^ d) for i in range(count)])  103 us
    ppermute x41, starting transfers between devices, exchange(): lax.ppermute(chunks[d // stride], axis, [(i, i ^ d) for i in range(count)])  57.3 us
    all_to_all x4, starting transfers between devices, swap(): return lax.all_to_all(x, axis, split_axis=0, concat_axis=0, tiled=True)  18.1 us
    all_gather x1, blocking collectives, local(): first = lax.all_gather(packed[:, :, :cols], 'fsdp', axis=0, tiled=True)  12.9 us
    all_to_all x4, waiting for transfers between devices, swap(): return lax.all_to_all(x, axis, split_axis=0, concat_axis=0, tiled=True)  7.53 us
    unnamed x54, local copies, waits for them, and re-layouts  7.14 us
  transfers between devices with their start and end apart: 47, of which 18 were waited for; matrix products, arithmetic and copies ran while one was open for 2% of the time, Pallas kernels for 29%

commit v1 on v0

--- a/solution.py
+++ b/solution.py
@@ -97,9 +97,9 @@
     pack_ref[rows:, span : 2 * span] = jnp.concatenate([low, jnp.zeros_like(low)], axis=0)
 
 
-def table_body(experts, me_ref, *refs):
-    blocks = refs[:-4]
-    pos_ref, gate_ref, stat_ref, all_ref = refs[-4:]
+def table_body(experts, capacity, me_ref, *refs):
+    blocks = refs[:-3]
+    table_ref, stat_ref, all_ref = refs[-3:]
     count = len(blocks)
     rows = blocks[0].shape[0] - 2 * INFO
     for d in range(count):
@@ -110,51 +110,64 @@
         wide = jnp.concatenate([values, jnp.zeros((rows - INFO, rows), F32)], axis=0)
         stat_ref[me_ref[1] ^ d] = wide.T
     flat = jnp.concatenate([all_ref[j] for j in range(count)], axis=1)
-    tokens = flat.shape[1]
     first, second = flat[0:1, :], flat[1:2, :]
     left, right = flat[2:3, :], flat[3:4, :]
     top = jnp.maximum(left, right)
     left, right = jnp.exp(left - top), jnp.exp(right - top)
     total = left + right
-    left, right = left / total, right / total
-    label = lax.broadcasted_iota(jnp.int32, (experts, tokens), 0).astype(F32)
+    earlier = lax.broadcasted_iota(jnp.int32, (rows, rows), 0) < lax.broadcasted_iota(
+        jnp.int32, (rows, rows), 1
+    )
+    earlier = jnp.where(earlier, 1.0, 0.0).astype(BF)
+    label = lax.broadcasted_iota(jnp.int32, (experts, flat.shape[1]), 0).astype(F32)
     is_first, is_second = label == first, label == second
-    hit = is_first | is_second
-    earlier = lax.broadcasted_iota(jnp.int32, (tokens, tokens), 0) < lax.broadcasted_iota(
-        jnp.int32, (tokens, tokens), 1
-    )
-    rank = mm(jnp.where(hit, 1.0, 0.0).astype(BF), jnp.where(earlier, 1.0, 0.0).astype(BF))
-    pos_ref[...] = jnp.where(hit, rank, -1.0)
-    gate_ref[...] = jnp.where(is_first, left, 0.0) + jnp.where(is_second, right, 0.0)
-
-
-def selection(pos_row, slots):
-    tokens = pos_row.shape[1]
-    slot = lax.broadcasted_iota(jnp.int32, (slots, tokens), 0).astype(F32)
-    return slot == pos_row
-
-
-def one_hot(pos_row, slots):
-    return jnp.where(selection(pos_row, slots), 1.0, 0.0).astype(BF)
-
-
-def dispatch_grad_body(experts, count, me_ref, pos_ref, gate_ref, *refs):
+    hit = jnp.where(is_first | is_second, 1.0, 0.0).astype(BF)
+    rank = jnp.concatenate(
+        [mm(hit[:, j * rows : (j + 1) * rows], earlier) for j in range(count)], axis=1
+    )
+    for k, (route, chosen) in enumerate(((first, is_first), (second, is_second))):
+        place = jnp.sum(jnp.where(chosen, rank, 0.0), axis=0, keepdims=True)
+        turned = (route.astype(jnp.int32) ^ me_ref[0]).astype(F32)
+        table_ref[k : k + 1, :] = turned * capacity + place
+        table_ref[2 + k : 3 + k, :] = route * capacity + place
+    table_ref[4:5, :] = left / total
+    table_ref[5:6, :] = right / total
+    table_ref[6:8, :] = jnp.zeros((2, flat.shape[1]), F32)
+
+
+def matches(table_ref, row, block, rows, slots):
+    slot = lax.broadcasted_iota(jnp.int32, (slots, rows), 0).astype(F32)
+    lanes = slice(block * rows, (block + 1) * rows)
+    return [slot == table_ref[row + k : row + k + 1, lanes] for k in range(2)]
+
+
+def one_hot(table_ref, row, block, rows, slots):
+    first, second = matches(table_ref, row, block, rows, slots)
+    return jnp.where(first | second, 1.0, 0.0).astype(BF)
+
+
+def gate_hot(table_ref, row, block, rows, slots):
+    first, second = matches(table_ref, row, block, rows, slots)
+    lanes = slice(block * rows, (block + 1) * rows)
+    return jnp.where(first, table_ref[4:5, lanes], 0.0) + jnp.where(
+        second, table_ref[5:6, lanes], 0.0
+    )
+
+
+def dispatch_grad_body(count, me_ref, table_ref, *refs):
     blocks = refs[:count]
     out_ref, tok_ref = refs[count:]
     rows = blocks[0].shape[0] - 2 * INFO
-    slots = out_ref.shape[1]
+    experts, slots, width = out_ref.shape
+    capacity = slots // count
     for d in range(count):
-        start = pl.multiple_of((me_ref[1] ^ d) * rows, rows)
-        tok_ref[pl.ds(start, rows), :] = blocks[d][:rows, :]
-
-    def step(e, carry):
-        chosen = selection(pos_ref[pl.ds(e, 1), :], slots)
-        pick = jnp.where(chosen, 1.0, 0.0).astype(BF)
-        gate = jnp.sum(jnp.where(chosen, gate_ref[pl.ds(e, 1), :], 0.0), axis=1, keepdims=True)
-        out_ref[e] = (mm(pick, tok_ref[...]) * gate).astype(BF)
-        return carry
-
-    lax.fori_loop(0, experts, step, 0)
+        tok_ref[me_ref[1] ^ d] = blocks[d][:rows, :]
+    for j in range(count):
+        pick = one_hot(table_ref, 2, j, rows, experts * capacity)
+        gate = gate_hot(table_ref, 2, j, rows, experts * capacity)
+        gate = jnp.sum(gate, axis=1, keepdims=True)
+        value = (mm(pick, tok_ref[j]) * gate).reshape(experts, capacity, width)
+        out_ref[:, j * capacity : (j + 1) * capacity, :] = value.astype(BF)
 
 
 def attention_forward_body(heads, me_ref, gains_ref, w_ref, *refs):
@@ -311,12 +324,16 @@
     proj_ref[...] = proj
 
 
-def project_body(count, me_ref, pos_ref, hat_ref, stat_ref, x_ref, gains_ref, proj_ref, *refs):
-    heads = refs[:count]
-    res_ref, own_ref = refs[count : count + 2]
-    out_refs = refs[count + 2 : -2]
+def project_body(count, peers, me_ref, table_ref, hat_ref, stat_ref, x_ref, gains_ref, *refs):
+    heads, chunks = refs[:count], refs[count : count + peers]
+    res_ref, own_ref, proj_ref = refs[count + peers : count + peers + 3]
+    out_refs = refs[count + peers + 3 : -2]
     acc_ref, ffn_ref = refs[-2:]
     rows = x_ref.shape[0]
+    span = chunks[0].shape[0]
+    for d in range(peers):
+        start = pl.multiple_of((me_ref[0] ^ d) * span, span)
+        proj_ref[pl.ds(start, span), :] = chunks[d][...]
     group = heads[0].shape[1]
     for d in range(count):
         start = pl.multiple_of((me_ref[1] ^ d) * group, group)
@@ -332,22 +349,30 @@
             hat * gains_ref[2:3, :] + gains_ref[3:4, :]
         ).astype(BF)
     own_ref[...] = res_ref[me_ref[1]]
-    for d, out_ref in enumerate(out_refs):
-        pick = one_hot(pos_ref[pl.ds(me_ref[0] ^ d, 1), :], out_ref.shape[0])
-        out_ref[...] = mm(pick, ffn_ref[...]).astype(BF)
-
-
-def combine_grad_body(experts, me_ref, pos_ref, res_ref, cot_ref, gains_ref, proj_ref, *refs):
+    capacity = out_refs[0].shape[0] // count
+    for j in range(count):
+        pick = one_hot(table_ref, 0, j, rows, len(out_refs) * capacity)
+        value = mm(pick, ffn_ref[j * rows : (j + 1) * rows, :]).astype(BF)
+        for d, out_ref in enumerate(out_refs):
+            out_ref[j * capacity : (j + 1) * capacity, :] = value[
+                d * capacity : (d + 1) * capacity, :
+            ]
+
+
+def combine_grad_body(experts, me_ref, table_ref, res_ref, cot_ref, gains_ref, proj_ref, *refs):
     back = refs[:experts]
     dx_ref, mix_ref, sums_ref, keep_ref = refs[experts : experts + 4]
-    send = refs[experts + 4 : -1]
-    part_ref = refs[-1]
-    slots = back[0].shape[0]
-    parts, rows, width = part_ref.shape
-    for d in range(experts):
-        pick = one_hot(pos_ref[pl.ds(me_ref[0] ^ d, 1), :], slots)
-        piece = mm_tn(pick, back[d][...]).reshape(parts, rows, width)
-        part_ref[...] = piece if d == 0 else part_ref[...] + piece
+    send = refs[experts + 4 : -2]
+    part_ref, line_ref = refs[-2:]
+    parts, rows, _ = part_ref.shape
+    capacity = back[0].shape[0] // parts
+    for j in range(parts):
+        for d in range(experts):
+            line_ref[j, d * capacity : (d + 1) * capacity, :] = back[d][
+                j * capacity : (j + 1) * capacity, :
+            ]
+        pick = one_hot(table_ref, 0, j, rows, experts * capacity)
+        part_ref[j] = mm_tn(pick, line_ref[j])
     sums_ref[...] = jnp.zeros(sums_ref.shape, F32)
     for j in range(parts):
         dy = part_ref[j]
@@ -368,33 +393,33 @@
             send[d - 1][...] = piece.astype(BF)
 
 
-def combine_out_body(experts, me_ref, pos_ref, gate_ref, back_ref, res_ref, own_ref, *refs):
+def combine_out_body(me_ref, table_ref, back_ref, res_ref, own_ref, *refs):
     send, part_ref = refs[:-1], refs[-1]
-    slots = back_ref.shape[1]
-    parts, rows, width = part_ref.shape
-    part_ref[...] = jnp.zeros(part_ref.shape, F32)
-
-    def step(e, carry):
-        chosen = selection(pos_ref[pl.ds(e, 1), :], slots)
-        gate = jnp.where(chosen, gate_ref[pl.ds(e, 1), :], 0.0)
+    experts, slots, width = back_ref.shape
+    parts, rows, _ = part_ref.shape
+    capacity = slots // parts
+    for j in range(parts):
+        back = back_ref[:, j * capacity : (j + 1) * capacity, :].reshape(experts * capacity, width)
+        gate = gate_hot(table_ref, 2, j, rows, experts * capacity)
         high = gate.astype(BF)
         low = (gate - high.astype(F32)).astype(BF)
-        piece = mm_tn(high, back_ref[e]) + mm_tn(low, back_ref[e])
-        part_ref[...] += piece.reshape(parts, rows, width)
-        return carry
-
-    lax.fori_loop(0, experts, step, 0)
+        part_ref[j] = mm_tn(high, back) + mm_tn(low, back)
     spread_parts(me_ref[1], part_ref, own_ref, send)
     own_ref[...] += res_ref[...]
 
 
-def hidden_grad_body(per, me_ref, g_ref, down_ref, *out_refs):
+def peer_groups(count):
+    quarter = count // 4
+    half = quarter // 2
+    own, near, far, both = [list(range(g * quarter, (g + 1) * quarter)) for g in range(4)]
+    return [own, both, far[:half] + near[:half], far[half:] + near[half:]]
+
+
+def hidden_grad_body(groups, me_ref, g_ref, down_ref, *out_refs):
     rows = g_ref.shape[1]
-    for g, out_ref in enumerate(out_refs):
-        for i in range(per):
-            out_ref[i * rows : (i + 1) * rows, :] = mm(
-                g_ref[me_ref[0] ^ (g * per + i)], down_ref[...]
-            )
+    for group, out_ref in zip(groups, out_refs):
+        for i, d in enumerate(group):
+            out_ref[i * rows : (i + 1) * rows, :] = mm(g_ref[me_ref[0] ^ d], down_ref[...])
 
 
 def expert_body(count, *refs):
@@ -423,12 +448,12 @@
         gr_refs[i][...] = mm_nt(gp_ref[i * rows : (i + 1) * rows, :], up_ref[...]).astype(BF)
 
 
-def expert_out_body(per, me_ref, down_ref, *refs):
+def expert_out_body(groups, me_ref, down_ref, *refs):
     hids, out_ref = refs[:-1], refs[-1]
     rows = out_ref.shape[1]
-    for g, hid_ref in enumerate(hids):
-        for i in range(per):
-            out_ref[me_ref[0] ^ (g * per + i)] = mm_nt(
+    for group, hid_ref in zip(groups, hids):
+        for i, d in enumerate(group):
+            out_ref[me_ref[0] ^ d] = mm_nt(
                 hid_ref[i * rows : (i + 1) * rows, :], down_ref[...]
             ).astype(BF)
 
@@ -444,13 +469,12 @@
         out_ref[0] = piece if g == 0 else out_ref[0] + piece
 
 
-def grad_down_body(count, me_ref, left_ref, *refs):
-    rights, out_ref, temp_ref = refs[:count], refs[count], refs[count + 1]
+def grad_down_body(groups, me_ref, left_ref, *refs):
+    rights, out_ref, temp_ref = refs[:-2], refs[-2], refs[-1]
     rows = left_ref.shape[1]
-    per = left_ref.shape[0] // count
-    for g in range(count):
-        for i in range(per):
-            temp_ref[i * rows : (i + 1) * rows, :] = left_ref[me_ref[0] ^ (g * per + i)]
+    for g, group in enumerate(groups):
+        for i, d in enumerate(group):
+            temp_ref[i * rows : (i + 1) * rows, :] = left_ref[me_ref[0] ^ d]
         piece = mm_tn(temp_ref[...], rights[g][...])
         out_ref[0] = piece if g == 0 else out_ref[0] + piece
 
@@ -480,8 +504,8 @@
     cols = 3 * group
     hidden = expert_up.shape[2]
     me = jnp.stack([lax.axis_index("fsdp"), lax.axis_index("seq")]).astype(jnp.int32)
-    groups = 4
-    per = nf // groups
+    groups = peer_groups(nf)
+    per = len(groups[0])
     bf_block = ((tok, width), BF)
 
     by_group = qkv_weight.reshape(wrows, 3, ns, group).transpose(2, 0, 1, 3).reshape(ns, wrows, cols)
@@ -499,12 +523,13 @@
     hat_own, cot_pack = kernel_call(
         prepare_body, [bf_block, ((tok + 2 * INFO, width), BF)], (inputs, cotangent, info)
     )
+    cot_pack, packed = lax.optimization_barrier((cot_pack, packed))
     cot_blocks = exchange([cot_pack] * ns, "seq", ns)
+    hat_blocks = exchange([hat_own] * ns, "seq", ns)
     first = lax.all_gather(packed[:, :, :cols], "fsdp", axis=0, tiled=True)
-    hat_own, proj_rows, me_late, first = lax.optimization_barrier(
-        (hat_own, packed[:, :wrows, cols:].reshape(ns * wrows, width), me, first)
-    )
-    hat_blocks = exchange([hat_own] * ns, "seq", ns)
+    proj_rows, first = lax.optimization_barrier(
+        (packed[:, :wrows, cols:].reshape(ns * wrows, width), first)
+    )
     qkv_w = first[:, :wrows].reshape(width, cols)
     gains = (
         first[:, wrows, : 4 * wrows]
@@ -513,22 +538,23 @@
         .reshape(4, width)
         .astype(F32)
     )
-    proj = swap(jnp.broadcast_to(proj_rows[None], (nf, ns * wrows, width)), "fsdp")
-    proj = proj.reshape(width, width)
-
-    pos, gate, stats = kernel_call(
-        functools.partial(table_body, nf),
-        [((nf, length), F32), ((nf, length), F32), ((ns, tok, tok), F32)],
-        (me_late, *cot_blocks),
+    proj_chunks = []
+    for piece in exchange([proj_rows] * (nf // 2), "fsdp", nf, stride=2):
+        proj_chunks += [piece, lax.ppermute(piece, "fsdp", [(i, i ^ 1) for i in range(nf)])]
+
+    table, stats = kernel_call(
+        functools.partial(table_body, nf, slots // ns),
+        [((8, length), F32), ((ns, tok, tok), F32)],
+        (after(me, qkv_w, gains), *cot_blocks),
         smem=1,
         scratch=[pltpu.VMEM((ns, INFO, tok), F32)],
     )
     (grad_sent,) = kernel_call(
-        functools.partial(dispatch_grad_body, nf, ns),
+        functools.partial(dispatch_grad_body, ns),
         [((nf, slots, width), BF)],
-        (me, pos, gate, *cot_blocks),
-        smem=1,
-        scratch=[pltpu.VMEM((length, width), BF)],
+        (me, table, *cot_blocks),
+        smem=1,
+        scratch=[pltpu.VMEM((ns, tok, width), BF)],
     )
     grad_in = swap(grad_sent, "fsdp")
     up, down = expert_up[0], expert_down[0]
@@ -547,42 +573,44 @@
     )
     heads_all = exchange([heads_s] * ns, "seq", ns)
     grad_hidden = kernel_call(
-        functools.partial(hidden_grad_body, per),
-        [((per * slots, hidden), F32)] * groups,
+        functools.partial(hidden_grad_body, groups),
+        [((per * slots, hidden), F32)] * len(groups),
         (me, grad_in, down),
         smem=1,
     )
-    res_all, residual, *sent = kernel_call(
-        functools.partial(project_body, ns),
-        [((ns, tok, width), F32), ((tok, width), F32)] + [((slots, width), BF)] * nf,
-        (me, pos, hat, stats, inputs, gains, proj, *heads_all),
+    res_all, residual, proj, *sent = kernel_call(
+        functools.partial(project_body, ns, nf),
+        [((ns, tok, width), F32), ((tok, width), F32), ((width, width), BF)]
+        + [((slots, width), BF)] * nf,
+        (me, table, hat, stats, inputs, gains, *heads_all, *proj_chunks),
         smem=1,
         scratch=[pltpu.VMEM((length, width), F32), pltpu.VMEM((length, width), BF)],
     )
     rows_in = exchange(sent, "fsdp", nf)
-    grad_rows, hid, grad_pre = [], [], []
-    for g in range(groups):
+    grad_rows, hid, grad_pre = [None] * nf, [], []
+    for g, group_ds in enumerate(groups):
         res = kernel_call(
             functools.partial(expert_body, per),
             [((slots, width), BF)] * per + [((per * slots, hidden), BF)] * 2,
-            (*rows_in[g * per : (g + 1) * per], grad_hidden[g], up),
+            (*[rows_in[d] for d in group_ds], grad_hidden[g], up),
             scratch=[pltpu.VMEM((per * slots, hidden), F32)],
         )
-        grad_rows += res[:per]
+        for d, piece in zip(group_ds, res):
+            grad_rows[d] = piece
         hid.append(res[per])
         grad_pre.append(res[per + 1])
     grad_back = exchange(grad_rows, "fsdp", nf)
     (expert_out,) = kernel_call(
-        functools.partial(expert_out_body, per),
+        functools.partial(expert_out_body, groups),
         [((nf, slots, width), BF)],
         (me, down, *hid),
         smem=1,
     )
     temp = [pltpu.VMEM((per * slots, width), BF)]
     (grad_up,) = kernel_call(
-        functools.partial(grad_up_body, groups),
+        functools.partial(grad_up_body, len(groups)),
         [((1, width, hidden), F32)],
-        (*rows_in, *grad_pre),
+        (*[rows_in[d] for group_ds in groups for d in group_ds], *grad_pre),
         scratch=temp,
     )
     (grad_down,) = kernel_call(
@@ -604,11 +632,11 @@
             ((length, group), F32),
         ]
         + [((length, group), BF)] * (ns - 1),
-        (me, pos, res_all, cotangent, gains, proj, *grad_back),
-        smem=1,
-        scratch=image,
-    )
-    out_back = swap(after(expert_out, gh_own), "fsdp")
+        (me, table, res_all, cotangent, gains, proj, *grad_back),
+        smem=1,
+        scratch=image + [pltpu.VMEM((ns, nf * slots // ns, width), BF)],
+    )
+    out_back = swap(after(expert_out, grad_down), "fsdp")
     gh_got = exchange([None] + gh_sent, "seq", ns)[1:]
     grad_qkv, sums_one, grad_own, *grad_share = kernel_call(
         functools.partial(attention_backward_body, heads),
@@ -661,11 +689,7 @@
     )
     tiny = line[0, : 4 * wrows].reshape(4, wrows)
     output, *out_share = kernel_call(
-        functools.partial(combine_out_body, nf),
-        share,
-        (me, pos, gate, out_back, residual),
-        smem=1,
-        scratch=image,
+        combine_out_body, share, (me, table, out_back, residual), smem=1, scratch=image
     )
     for piece in exchange([None] + out_share, "seq", ns)[1:]:
         output = output + piece.astype(F32)

time: 337 us -> 380 us (1.13)
  waiting for transfers between devices: 110 us -> 151 us
  Pallas kernels: 111 us -> 116 us
    ppermute x41 -> x44, waiting for transfers between devices: 103 us -> 143 us  [exchange(): lax.ppermute(chunks[d // stride], axis, [(i, i ^ d) for i in range(count)])]
    pallas_call x22, Pallas kernels: 111 us -> 116 us  [kernel_call(): pl.pallas_call(body, out_shape=[jax.ShapeDtypeStruct(s, d) for s, d in ou...]
    ppermute x41 -> x44, starting transfers between devices: 57.3 us -> 62.2 us  [exchange(): lax.ppermute(chunks[d // stride], axis, [(i, i ^ d) for i in range(count)])]
    all_to_all x4 -> x3, starting transfers between devices: 18.1 us -> 14.3 us  [swap(): return lax.all_to_all(x, axis, split_axis=0, concat_axis=0, tiled=True)]
  transfers between devices with their start and end apart: 47 -> 53, of which waited for: 18 -> 18; matrix products, arithmetic and copies ran while one was open for 2% -> 2% of each run, Pallas kernels for 29% -> 23%
where the time goes in v1:
time: 380 us; the launch traced here: 376 us
  waiting for transfers between devices  151 us (40%)
  Pallas kernels  116 us (31%)
  starting transfers between devices  77.4 us (20%)
  local copies, waits for them, and re-layouts  12.4 us (3%)
  blocking collectives  12.1 us (3%)
  other arithmetic  6.06 us (2%)
    ppermute x44, waiting for transfers between devices, exchange(): lax.ppermute(chunks[d // stride], axis, [(i, i ^ d) for i in range(count)])  143 us
    pallas_call x22, Pallas kernels, kernel_call(): pl.pallas_call(body, out_shape=[jax.ShapeDtypeStruct(s, d) for s, d in ou...  116 us
    ppermute x44, starting transfers between devices, exchange(): lax.ppermute(chunks[d // stride], axis, [(i, i ^ d) for i in range(count)])  62.2 us
    all_to_all x3, starting transfers between devices, swap(): return lax.all_to_all(x, axis, split_axis=0, concat_axis=0, tiled=True)  14.3 us
    all_gather x1, blocking collectives, local(): first = lax.all_gather(packed[:, :, :cols], 'fsdp', axis=0, tiled=True)  12.1 us
  transfers between devices with their start and end apart: 53, of which 18 were waited for; matrix products, arithmetic and copies ran while one was open for 2% of the time, Pallas kernels for 23%

profile of v1, /device:TPU:0, one launch (start us, length us, event | category | flops | bytes accessed | tf_op | source)
XLA Modules:
  0.0 376.0 jit_solution(5717439807226675759)
XLA Ops:
  4.4 6.3 %all-to-all-start = ((bf16[4,25,1344]{2,1,0:T(8,128)(2,1)}), bf16[4,25,1344]{2,1,0:T(8,128)(2,1)S(1)}, u32[]{:S(2)}, u32[]{:S(2)}) async-start(bf16[4,25,1344]{2,1,0:T(8,128)(2,1)} %fusion), calls=%async_computation | async-start | bytes 720896 | tf_op jit(solution)/shard_map/all_to_all | solution.py:51
  14.2 7.5 %all-to-all-done = bf16[4,25,1344]{2,1,0:T(8,128)(2,1)S(1)} async-done(((bf16[4,25,1344]{2,1,0:T(8,128)(2,1)}), bf16[4,25,1344]{2,1,0:T(8,128)(2,1)S(1)}, u32[]{:S(2)}, u32[]{:S(2)}) %all-to-all-start) | async-done | bytes 268832 | tf_op jit(solution)/shard_map/all_to_all | solution.py:51
  26.4 12.1 %all_gather.3 = bf16[32,25,576]{2,1,0:T(8,128)(2,1)S(1)} all-gather(bf16[4,25,576]{2,1,0:T(8,128)(2,1)S(1)} %slice.34), channel_id=1, replica_groups=mesh['fsdp'=8,'seq'=4] {'fsdp'}, dimensions={0}, use_global_device_ids=true | all-gather | bytes 1036800 | tf_op jit(solution)/shard_map/all_gather | solution.py:529
  62.7 8.8 %collective-permute-done.4.refs_2_ = bf16[128,768]{1,0:T(8,128)(2,1)S(1)} collective-permute-done((bf16[128,768]{1,0:T(8,128)(2,1)S(1)}, bf16[128,768]{1,0:T(8,128)(2,1)S(1)}, u32[]{:S(2)}, u32[]{:S(2)}) %collective-permute-start.4) | collective-permute-done | bytes 196640 | tf_op jit(solution)/shard_map/ppermute | solution.py:46
  80.9 13.7 %collective-permute-done.14.refs_10_ = bf16[96,768]{1,0:T(8,128)(2,1)} collective-permute-done((bf16[96,768]{1,0:T(8,128)(2,1)S(1)}, bf16[96,768]{1,0:T(8,128)(2,1)}, u32[]{:S(2)}, u32[]{:S(2)}) %collective-permute-start.14) | collective-permute-done | bytes 147488 | tf_op jit(solution)/shard_map/ppermute | solution.py:46
  97.6 10.3 %collective-permute-done.7.refs_2_ = bf16[512,192]{1,0:T(8,128)(2,1)} collective-permute-done((bf16[512,192]{1,0:T(8,128)(2,1)}, bf16[512,192]{1,0:T(8,128)(2,1)}, u32[]{:S(2)}, u32[]{:S(2)}) %collective-permute-start.7) | collective-permute-done | bytes 196640 | tf_op jit(solution)/shard_map/ppermute | solution.py:46
  110.5 6.7 %shard_map.198 = (f32[4,128,768]{2,1,0:T(8,128)}, f32[128,768]{1,0:T(8,128)}, bf16[768,768]{1,0:T(8,128)(2,1)}, bf16[256,768]{1,0:T(8,128)(2,1)}, bf16[256,768]{...) custom-call(s32[2]{0:T(128)} %pad_add_fusion.me_ref.refs_0_, ...), custom_call_target="tpu_custom_call" | custom-call | tf_op jit(solution)/shard_map/pallas_call | solution.py:34
  133.6 6.1 %shard_map.200 = (f32[512,768]{1,0:T(8,128)}, f32[512,768]{1,0:T(8,128)}, f32[512,768]{1,0:T(8,128)}, f32[512,768]{1,0:T(8,128)}) custom-call(s32[2]{0:T(128)} %pad_add_fusion.me_ref.refs_0_, bf16[8,256,768]{2,1,0:T(8,128)(2,1)} %copy-done, bf16[768,768]{1,0:T(8,128)(2,1)} %bitcast.24), custom_call_target="tpu_custom_call" | custom-call | tf_op jit(solution)/shard_map/pallas_call | solution.py:34
  139.7 5.8 %shard_map.201 = (bf16[256,768]{1,0:T(8,128)(2,1)}, bf16[256,768]{1,0:T(8,128)(2,1)}, bf16[512,768]{1,0:T(8,128)(2,1)}, bf16[512,768]{1,0:T(8,128)(2,1)}) custom-call(bf16[256,768]{1,0:T(8,128)(2,1)} %get-tuple-element.103.refs_0_, bf16[256,768]{1,0:T(8,128)(2,1)} %copy-done.2, f32[512,768]{1,0:T(8,128)} %get-tuple-element.105.refs_2_, bf16[768,768]{1,0:T(8,128)(2,1)} %bitcast.18), custom_call_target="tpu_custom_call" | custom-call | tf_op jit(solution)/shard_map/pallas_call | solution.py:34
  145.5 5.8 %shard_map.204 = (bf16[256,768]{1,0:T(8,128)(2,1)}, bf16[256,768]{1,0:T(8,128)(2,1)}, bf16[512,768]{1,0:T(8,128)(2,1)}, bf16[512,768]{1,0:T(8,128)(2,1)}) custom-call(bf16[256,768]{1,0:T(8,128)(2,1)} %copy-done.3, bf16[256,768]{1,0:T(8,128)(2,1)} %collective-permute-done.22.refs_1_.refs_7_, f32[512,768]{1,0:T(8,128)} %get-tuple-element.117.refs_2_, ...), custom_call_target="tpu_custom_call" | custom-call | tf_op jit(solution)/shard_map/pallas_call | solution.py:34
  151.2 18.4 %shard_map.203 = (bf16[256,768]{1,0:T(8,128)(2,1)}, bf16[256,768]{1,0:T(8,128)(2,1)}, bf16[512,768]{1,0:T(8,128)(2,1)}, bf16[512,768]{1,0:T(8,128)(2,1)}) custom-call(bf16[256,768]{1,0:T(8,128)(2,1)} %collective-permute-done.19.refs_0_.refs_4_, bf16[256,768]{1,0:T(8,128)(2,1)} %collective-permute-done.20.refs_1_.refs_5_, ...), custom_call_target="tpu_custom_call" | custom-call | tf_op jit(solution)/shard_map/pallas_call | solution.py:34
  169.6 5.8 %shard_map.202 = (bf16[256,768]{1,0:T(8,128)(2,1)}, bf16[256,768]{1,0:T(8,128)(2,1)}, bf16[512,768]{1,0:T(8,128)(2,1)}, bf16[512,768]{1,0:T(8,128)(2,1)}) custom-call(bf16[256,768]{1,0:T(8,128)(2,1)} %collective-permute-done.17.refs_0_.refs_2_, bf16[256,768]{1,0:T(8,128)(2,1)} %collective-permute-done.18.refs_1_.refs_3_, ...), custom_call_target="tpu_custom_call" | custom-call | tf_op jit(solution)/shard_map/pallas_call | solution.py:34
  175.4 6.5 %shard_map.205 = bf16[8,256,768]{2,1,0:T(8,128)(2,1)} custom-call(s32[2]{0:T(128)} %pad_add_fusion.me_ref.refs_0_, bf16[768,768]{1,0:T(8,128)(2,1)} %bitcast.25, bf16[512,768]{1,0:T(8,128)(2,1)} %get-tuple-element.106.refs_0_, bf16[512,768]{1,0:T(8,128)(2,1)} %get-tuple-element.110.refs_1_, bf16[512,768]{1,0:T(8,128)(2,1)} %get-tuple-element.114.refs_2_, ...), custom_call_target="tpu_custom_call" | custom-call | tf_op jit(solution)/shard_map/pallas_call | solution.py:34
  181.9 6.9 %shard_map.206 = f32[1,768,768]{2,1,0:T(8,128)} custom-call(s32[2]{0:T(128)} %pad_add_fusion.me_ref.refs_0_, bf16[8,256,768]{2,1,0:T(8,128)(2,1)} %copy-done, bf16[512,768]{1,0:T(8,128)(2,1)} %get-tuple-element.106.refs_0_, bf16[512,768]{1,0:T(8,128)(2,1)} %get-tuple-element.110.refs_1_, bf16[512,768]{1,0:T(8,128)(2,1)} %get-tuple-element.114.refs_2_, ...), custom_call_target="tpu_custom_call" | custom-call | tf_op jit(solution)/shard_map/pallas_call | solution.py:34
  199.1 38.1 %collective-permute-done.28.refs_3_ = bf16[256,768]{1,0:T(8,128)(2,1)} collective-permute-done((bf16[256,768]{1,0:T(8,128)(2,1)}, bf16[256,768]{1,0:T(8,128)(2,1)}, u32[]{:S(2)}, u32[]{:S(2)}) %collective-permute-start.28) | collective-permute-done | bytes 393248 | tf_op jit(solution)/shard_map/ppermute | solution.py:46
  239.6 7.2 %collective-permute-done.27.refs_2_ = bf16[256,768]{1,0:T(8,128)(2,1)} collective-permute-done((bf16[256,768]{1,0:T(8,128)(2,1)}, bf16[256,768]{1,0:T(8,128)(2,1)}, u32[]{:S(2)}, u32[]{:S(2)}) %collective-permute-start.27) | collective-permute-done | bytes 393248 | tf_op jit(solution)/shard_map/ppermute | solution.py:46
  246.8 9.3 %collective-permute-done.31.refs_6_ = bf16[256,768]{1,0:T(8,128)(2,1)} collective-permute-done((bf16[256,768]{1,0:T(8,128)(2,1)}, bf16[256,768]{1,0:T(8,128)(2,1)}, u32[]{:S(2)}, u32[]{:S(2)}) %collective-permute-start.31) | collective-permute-done | bytes 393248 | tf_op jit(solution)/shard_map/ppermute | solution.py:46
  256.2 7.3 %collective-permute-done.32.refs_7_ = bf16[256,768]{1,0:T(8,128)(2,1)} collective-permute-done((bf16[256,768]{1,0:T(8,128)(2,1)}, bf16[256,768]{1,0:T(8,128)(2,1)}, u32[]{:S(2)}, u32[]{:S(2)}) %collective-permute-start.32) | collective-permute-done | bytes 393248 | tf_op jit(solution)/shard_map/ppermute | solution.py:46
  263.5 6.1 %shard_map.208 = (f32[4,128,768]{2,1,0:T(8,128)}, bf16[512,768]{1,0:T(8,128)(2,1)}, f32[2,768]{1,0:T(2,128)}, f32[512,192]{1,0:T(8,128)}, bf16[512,192]{1,0:T(8,...) custom-call(s32[2]{0:T(128)} %pad_add_fusion.me_ref.refs_0_, f32[8,512]{1,0:T(8,128)} %get-tuple-element.97.table_ref, ...), custom_call_target="tpu_custom_call" | custom-call | tf_op jit(solution)/shard_map/pallas_call | solution.py:34
  278.0 8.9 %collective-permute-done.33.refs_2_ = bf16[512,192]{1,0:T(8,128)(2,1)S(1)} collective-permute-done((bf16[512,192]{1,0:T(8,128)(2,1)}, bf16[512,192]{1,0:T(8,128)(2,1)S(1)}, u32[]{:S(2)}, u32[]{:S(2)}) %collective-permute-start.33) | collective-permute-done | bytes 196640 | tf_op jit(solution)/shard_map/ppermute | solution.py:46
  287.0 8.3 %collective-permute-done.34.refs_3_ = bf16[512,192]{1,0:T(8,128)(2,1)} collective-permute-done((bf16[512,192]{1,0:T(8,128)(2,1)}, bf16[512,192]{1,0:T(8,128)(2,1)}, u32[]{:S(2)}, u32[]{:S(2)}) %collective-permute-start.34) | collective-permute-done | bytes 196640 | tf_op jit(solution)/shard_map/ppermute | solution.py:46
  295.3 8.0 %shard_map.209 = (bf16[512,576]{1,0:T(8,128)(2,1)}, f32[2,768]{1,0:T(2,128)}, f32[128,768]{1,0:T(8,128)}, bf16[128,768]{1,0:T(8,128)(2,1)}, bf16[128,768]{1,0:T(8,128)(2,1)}, /*index=5*/bf16[128,768]{1,0:T(8,128)(2,1)}) custom-call(s32[2]{0:T(128)} %pad_add_fusion.me_ref.refs_0_, f32[512,192]{1,0:T(8,128)} %get-tuple-element.135.refs_1_, ...), custom_call_target="tpu_custom_call" | custom-call | tf_op jit(solution)/shard_map/pallas_call | solution.py:34
  326.4 7.1 %shard_map.216 = f32[1,768,768]{2,1,0:T(8,128)} custom-call(bf16[256,768]{1,0:T(8,128)(2,1)} %get-tuple-element.103.refs_0_, bf16[256,768]{1,0:T(8,128)(2,1)} %copy-done.2, bf16[256,768]{1,0:T(8,128)(2,1)} %collective-permute-done.17.refs_0_.refs_2_, bf16[256,768]{1,0:T(8,128)(2,1)} %collective-permute-done.18.refs_1_.refs_3_, ...), custom_call_target="tpu_custom_call" | custom-call | tf_op jit(solution)/shard_map/pallas_call | solution.py:34
  364.5 9.4 %collective-permute-done.24 = bf16[128,768]{1,0:T(8,128)(2,1)S(1)} collective-permute-done((bf16[128,768]{1,0:T(8,128)(2,1)}, bf16[128,768]{1,0:T(8,128)(2,1)S(1)}, u32[]{:S(2)}, u32[]{:S(2)}) %collective-permute-start.24) | collective-permute-done | bytes 196640 | tf_op jit(solution)/shard_map/ppermute | solution.py:46
  (179 shorter events, 144.6 us)
Async XLA Ops:
  21.9 18.4 %collective-permute-start.2 = (bf16[144,768]{1,0:T(8,128)(2,1)}, bf16[144,768]{1,0:T(8,128)(2,1)S(1)}, u32[]{:S(2)}, u32[]{:S(2)}) collective-permute-start(bf16[144,768]{1,0:T(8,128)(2,1)} %get-tuple-element.96.refs_0_), channel_id=1, source_target_pairs={{0,3},{1,2},{2,1},{3,0},{4,7},{5,6},{6,5},{7,4},{8,11},{9,10},{10,... | collective-permute-start | bytes 663560 | tf_op jit(solution)/shard_map/ppermute | solution.py:46
  23.4 17.7 %collective-permute-start = (bf16[144,768]{1,0:T(8,128)(2,1)}, bf16[144,768]{1,0:T(8,128)(2,1)S(1)}, u32[]{:S(2)}, u32[]{:S(2)}) collective-permute-start(bf16[144,768]{1,0:T(8,128)(2,1)} %get-tuple-element.96.refs_0_), channel_id=1, source_target_pairs={{0,1},{1,0},{2,3},{3,2},{4,5},{5,4},{6,7},{7,6},{8,9},{9,8},{10,11... | collective-permute-start | bytes 663560 | tf_op jit(solution)/shard_map/ppermute | solution.py:46
  48.6 83.4 %all-to-all-start.1 = ((bf16[8,256,768]{2,1,0:T(8,128)(2,1)}), bf16[8,256,768]{2,1,0:T(8,128)(2,1)S(1)}, u32[]{:S(2)}, u32[]{:S(2)}) async-start(bf16[8,256,768]{2,1,0:T(8,128)(2,1)} %shard_map.199), calls=%async_computation.1 | async-start | bytes 6291456 | tf_op jit(solution)/shard_map/all_to_all | solution.py:51
  57.3 37.2 %collective-permute-start.14 = (bf16[96,768]{1,0:T(8,128)(2,1)S(1)}, bf16[96,768]{1,0:T(8,128)(2,1)}, u32[]{:S(2)}, u32[]{:S(2)}) collective-permute-start(bf16[96,768]{1,0:T(8,128)(2,1)S(1)} %bitcast.27), channel_id=1, source_target_pairs={{0,24},{4,28},{8,16},{12,20},{16,8},{20,12},{24,0},{28,4},{1,25},{... | collective-permute-start | bytes 442376 | tf_op jit(solution)/shard_map/ppermute | solution.py:46
  60.3 35.9 %collective-permute-start.12 = (bf16[96,768]{1,0:T(8,128)(2,1)S(1)}, bf16[96,768]{1,0:T(8,128)(2,1)}, u32[]{:S(2)}, u32[]{:S(2)}) collective-permute-start(bf16[96,768]{1,0:T(8,128)(2,1)S(1)} %bitcast.28), channel_id=1, source_target_pairs={{0,16},{4,20},{8,24},{12,28},{16,0},{20,4},{24,8},{28,12},{1,17},{... | collective-permute-start | bytes 442376 | tf_op jit(solution)/shard_map/ppermute | solution.py:46
  77.3 20.2 %collective-permute-start.8 = (bf16[512,192]{1,0:T(8,128)(2,1)}, bf16[512,192]{1,0:T(8,128)(2,1)S(1)}, u32[]{:S(2)}, u32[]{:S(2)}) collective-permute-start(bf16[512,192]{1,0:T(8,128)(2,1)} %get-tuple-element.101.refs_0_), channel_id=1, source_target_pairs={{0,3},{1,2},{2,1},{3,0},{4,7},{5,6},{6,5},{7,4},{8,11},{9,10},{10,... | collective-permute-start | bytes 589832 | tf_op jit(solution)/shard_map/ppermute | solution.py:46
  118.1 33.1 %collective-permute-start.19 = (bf16[256,768]{1,0:T(8,128)(2,1)}, bf16[256,768]{1,0:T(8,128)(2,1)}, u32[]{:S(2)}, u32[]{:S(2)}) collective-permute-start(bf16[256,768]{1,0:T(8,128)(2,1)} %get-tuple-element.111), channel_id=1, source_target_pairs={{0,16},{4,20},{8,24},{12,28},{16,0},{20,4},{24,8},{28,12},{1,17},{... | collective-permute-start | bytes 1179656 | tf_op jit(solution)/shard_map/ppermute | solution.py:46
  119.4 26.1 %collective-permute-start.22 = (bf16[256,768]{1,0:T(8,128)(2,1)}, bf16[256,768]{1,0:T(8,128)(2,1)}, u32[]{:S(2)}, u32[]{:S(2)}) collective-permute-start(bf16[256,768]{1,0:T(8,128)(2,1)} %get-tuple-element.116), channel_id=1, source_target_pairs={{0,12},{4,8},{8,4},{12,0},{16,28},{20,24},{24,20},{28,16},{1,13},{... | collective-permute-start | bytes 1179656 | tf_op jit(solution)/shard_map/ppermute | solution.py:46
  120.7 30.5 %collective-permute-start.20 = (bf16[256,768]{1,0:T(8,128)(2,1)}, bf16[256,768]{1,0:T(8,128)(2,1)}, u32[]{:S(2)}, u32[]{:S(2)}) collective-permute-start(bf16[256,768]{1,0:T(8,128)(2,1)} %get-tuple-element.112), channel_id=1, source_target_pairs={{0,8},{4,12},{8,0},{12,4},{16,24},{20,28},{24,16},{28,20},{1,9},{5... | collective-permute-start | bytes 1179656 | tf_op jit(solution)/shard_map/ppermute | solution.py:46
  121.3 48.3 %collective-permute-start.17 = (bf16[256,768]{1,0:T(8,128)(2,1)}, bf16[256,768]{1,0:T(8,128)(2,1)}, u32[]{:S(2)}, u32[]{:S(2)}) collective-permute-start(bf16[256,768]{1,0:T(8,128)(2,1)} %get-tuple-element.107), channel_id=1, source_target_pairs={{0,24},{4,28},{8,16},{12,20},{16,8},{20,12},{24,0},{28,4},{1,25},{... | collective-permute-start | bytes 1179656 | tf_op jit(solution)/shard_map/ppermute | solution.py:46
  129.1 40.5 %collective-permute-start.18 = (bf16[256,768]{1,0:T(8,128)(2,1)}, bf16[256,768]{1,0:T(8,128)(2,1)}, u32[]{:S(2)}, u32[]{:S(2)}) collective-permute-start(bf16[256,768]{1,0:T(8,128)(2,1)} %get-tuple-element.108), channel_id=1, source_target_pairs={{0,28},{4,24},{8,20},{12,16},{16,12},{20,8},{24,4},{28,0},{1,29},{... | collective-permute-start | bytes 1179656 | tf_op jit(solution)/shard_map/ppermute | solution.py:46
  188.7 160.2 %all-to-all-start.2 = ((bf16[8,256,768]{2,1,0:T(8,128)(2,1)}), bf16[8,256,768]{2,1,0:T(8,128)(2,1)S(1)}, u32[]{:S(2)}, u32[]{:S(2)}) async-start(bf16[8,256,768]{2,1,0:T(8,128)(2,1)} %shard_map.205), calls=%async_computation.2 | async-start | bytes 6291456 | tf_op jit(solution)/shard_map/all_to_all | solution.py:51
  192.8 44.5 %collective-permute-start.28 = (bf16[256,768]{1,0:T(8,128)(2,1)}, bf16[256,768]{1,0:T(8,128)(2,1)}, u32[]{:S(2)}, u32[]{:S(2)}) collective-permute-start(bf16[256,768]{1,0:T(8,128)(2,1)} %get-tuple-element.130), channel_id=1, source_target_pairs={{0,12},{4,8},{8,4},{12,0},{16,28},{20,24},{24,20},{28,16},{1,13},{... | collective-permute-start | bytes 1179656 | tf_op jit(solution)/shard_map/ppermute | solution.py:46
  194.4 45.2 %collective-permute-start.30 = (bf16[256,768]{1,0:T(8,128)(2,1)}, bf16[256,768]{1,0:T(8,128)(2,1)}, u32[]{:S(2)}, u32[]{:S(2)}) collective-permute-start(bf16[256,768]{1,0:T(8,128)(2,1)} %get-tuple-element.132), channel_id=1, source_target_pairs={{0,20},{4,16},{8,28},{12,24},{16,4},{20,0},{24,12},{28,8},{1,21},{... | collective-permute-start | bytes 1179656 | tf_op jit(solution)/shard_map/ppermute | solution.py:46
  195.6 51.2 %collective-permute-start.27 = (bf16[256,768]{1,0:T(8,128)(2,1)}, bf16[256,768]{1,0:T(8,128)(2,1)}, u32[]{:S(2)}, u32[]{:S(2)}) collective-permute-start(bf16[256,768]{1,0:T(8,128)(2,1)} %get-tuple-element.129), channel_id=1, source_target_pairs={{0,8},{4,12},{8,0},{12,4},{16,24},{20,28},{24,16},{28,20},{1,9},{5... | collective-permute-start | bytes 1179656 | tf_op jit(solution)/shard_map/ppermute | solution.py:46
  196.2 50.6 %collective-permute-start.29 = (bf16[256,768]{1,0:T(8,128)(2,1)}, bf16[256,768]{1,0:T(8,128)(2,1)}, u32[]{:S(2)}, u32[]{:S(2)}) collective-permute-start(bf16[256,768]{1,0:T(8,128)(2,1)} %get-tuple-element.131), channel_id=1, source_target_pairs={{0,16},{4,20},{8,24},{12,28},{16,0},{20,4},{24,8},{28,12},{1,17},{... | collective-permute-start | bytes 1179656 | tf_op jit(solution)/shard_map/ppermute | solution.py:46
  196.6 59.6 %collective-permute-start.31 = (bf16[256,768]{1,0:T(8,128)(2,1)}, bf16[256,768]{1,0:T(8,128)(2,1)}, u32[]{:S(2)}, u32[]{:S(2)}) collective-permute-start(bf16[256,768]{1,0:T(8,128)(2,1)} %get-tuple-element.133), channel_id=1, source_target_pairs={{0,24},{4,28},{8,16},{12,20},{16,8},{20,12},{24,0},{28,4},{1,25},{... | collective-permute-start | bytes 1179656 | tf_op jit(solution)/shard_map/ppermute | solution.py:46
  237.2 26.2 %collective-permute-start.32 = (bf16[256,768]{1,0:T(8,128)(2,1)}, bf16[256,768]{1,0:T(8,128)(2,1)}, u32[]{:S(2)}, u32[]{:S(2)}) collective-permute-start(bf16[256,768]{1,0:T(8,128)(2,1)} %get-tuple-element.134), channel_id=1, source_target_pairs={{0,28},{4,24},{8,20},{12,16},{16,12},{20,8},{24,4},{28,0},{1,29},{... | collective-permute-start | bytes 1179656 | tf_op jit(solution)/shard_map/ppermute | solution.py:46
  273.2 33.8 %collective-permute-start.43 = (bf16[4,96,768]{2,1,0:T(8,128)(2,1)}, bf16[4,96,768]{2,1,0:T(8,128)(2,1)}, u32[]{:S(2)}, u32[]{:S(2)}) collective-permute-start(bf16[4,96,768]{2,1,0:T(8,128)(2,1)} %get-tuple-element.158), channel_id=1, source_target_pairs={{0,4},{4,0},{8,12},{12,8},{16,20},{20,16},{24,28},{28,24},{1,5},{5... | collective-permute-start | bytes 1769480 | tf_op jit(solution)/shard_map/ppermute | solution.py:655
  273.6 21.7 %collective-permute-start.34 = (bf16[512,192]{1,0:T(8,128)(2,1)}, bf16[512,192]{1,0:T(8,128)(2,1)}, u32[]{:S(2)}, u32[]{:S(2)}) collective-permute-start(bf16[512,192]{1,0:T(8,128)(2,1)} %get-tuple-element.137), channel_id=1, source_target_pairs={{0,2},{1,3},{2,0},{3,1},{4,6},{5,7},{6,4},{7,5},{8,10},{9,11},{10,... | collective-permute-start | bytes 589832 | tf_op jit(solution)/shard_map/ppermute | solution.py:46
  276.0 19.3 %collective-permute-start.35 = (bf16[512,192]{1,0:T(8,128)(2,1)}, bf16[512,192]{1,0:T(8,128)(2,1)}, u32[]{:S(2)}, u32[]{:S(2)}) collective-permute-start(bf16[512,192]{1,0:T(8,128)(2,1)} %get-tuple-element.138), channel_id=1, source_target_pairs={{0,3},{1,2},{2,1},{3,0},{4,7},{5,6},{6,5},{7,4},{8,11},{9,10},{10,... | collective-permute-start | bytes 589832 | tf_op jit(solution)/shard_map/ppermute | solution.py:46
  315.6 22.8 %collective-permute-start.36 = (bf16[128,768]{1,0:T(8,128)(2,1)}, bf16[128,768]{1,0:T(8,128)(2,1)}, u32[]{:S(2)}, u32[]{:S(2)}) collective-permute-start(bf16[128,768]{1,0:T(8,128)(2,1)} %get-tuple-element.143), channel_id=1, source_target_pairs={{0,1},{1,0},{2,3},{3,2},{4,5},{5,4},{6,7},{7,6},{8,9},{9,8},{10,11... | collective-permute-start | bytes 589832 | tf_op jit(solution)/shard_map/ppermute | solution.py:46
  321.0 19.3 %collective-permute-start.37 = (bf16[128,768]{1,0:T(8,128)(2,1)}, bf16[128,768]{1,0:T(8,128)(2,1)}, u32[]{:S(2)}, u32[]{:S(2)}) collective-permute-start(bf16[128,768]{1,0:T(8,128)(2,1)} %get-tuple-element.144), channel_id=1, source_target_pairs={{0,2},{1,3},{2,0},{3,1},{4,6},{5,7},{6,4},{7,5},{8,10},{9,11},{10,... | collective-permute-start | bytes 589832 | tf_op jit(solution)/shard_map/ppermute | solution.py:46
  321.9 18.3 %collective-permute-start.38 = (bf16[128,768]{1,0:T(8,128)(2,1)}, bf16[128,768]{1,0:T(8,128)(2,1)}, u32[]{:S(2)}, u32[]{:S(2)}) collective-permute-start(bf16[128,768]{1,0:T(8,128)(2,1)} %get-tuple-element.145), channel_id=1, source_target_pairs={{0,3},{1,2},{2,1},{3,0},{4,7},{5,6},{6,5},{7,4},{8,11},{9,10},{10,... | collective-permute-start | bytes 589832 | tf_op jit(solution)/shard_map/ppermute | solution.py:46
  (55 other events, 604.6 us)
